TPU v7x, 256 devices: a whole 4x4x8 slice. The times are simulated.
256 devices in a mesh: vel: 4 (over y_hi, core), space: 64 (over z, x, y_lo).
Axes of the slice: x: 4, y: 4 (y_hi: 2, y_lo: 2; y = y_hi * 2 + y_lo), z: 8, core: 2. Of those that a mesh axis runs over, the one named last changes fastest.
Arguments:
- distribution: float32 [13824, 128, 128], P('vel', 'space'), may hold values from -4 to 4
- vel_index: int32 [13824], P('vel'), may hold values from 0 to 13823, as said below
- collision_time: float32 [128, 128], P('space'), may hold values from 0.5 to 4
- wall_flags: int32 [128, 128], P('space'), may hold values 0 or 1
- wall_temp: float32 [128, 128], P('space'), may hold values from -2 to 2
Outputs:
- distribution_new: float32 [13824, 128, 128], P('vel', 'space')
- correction: float32 [128, 128], P('space')
Inputs may be any that keep to these rules, and one draw needn't show every extreme that they name: `vel_index`: a permutation of 0 to 13823; in each aligned block of 13824 // 4 slots exactly half of the values have index_x >= 12.
All inputs are finite; a program needn't handle non-finite values. No bound on the sum of `wall_flags` on one device may be relied on, other than what follows from the above.
Results may differ from a plain program's by a relative error of at most 0.0003.
Values sent between devices are 32-bit elements; how exact they have to be, the bound alone decides.
No kernel may reach another device: no remote copies, remote signals or barrier semaphores. Data moves between devices by JAX's collectives and lax.ppermute only.
A program may use at most 64 MiB of HBM per device.

v0:
```python
import math

import jax
import jax.numpy as jnp
from jax import lax
from jax.sharding import PartitionSpec as P

VGRID = 24
ITERS = 3


VELOCITY_MAX = 4.5
COOLING = 0.08
SHAKHOV = 0.8 * (1.0 - 2.0 / 3.0)


def with_halo(shard, sides, width):
    for axis, dim in sides:
        peers, length = (lax.axis_size(axis), shard.shape[dim])
        up = [(i, (i + 1) % peers) for i in range(peers - 1)]
        down = [(j, i) for i, j in up]
        last = lax.slice_in_dim(shard, length - width, length, axis=dim)
        first = lax.slice_in_dim(shard, 0, width, axis=dim)
        before = lax.ppermute(last, axis, up)
        after = lax.ppermute(first, axis, down)
        shard = jnp.concatenate([before, shard, after], axis=dim)
    return shard


def velocity_tables(slot_ids):
    index_x = slot_ids // (VGRID * VGRID)
    index_y = slot_ids // VGRID % VGRID
    index_z = slot_ids % VGRID
    spacing = 2.0 * VELOCITY_MAX / VGRID
    speed_x = -VELOCITY_MAX + (index_x.astype(jnp.float32) + 0.5) * spacing
    speed_y = -VELOCITY_MAX + (index_y.astype(jnp.float32) + 0.5) * spacing
    speed_z = -VELOCITY_MAX + (index_z.astype(jnp.float32) + 0.5) * spacing
    speed_sq = speed_x * speed_x + speed_y * speed_y + speed_z * speed_z
    weight = spacing**3
    unity = jnp.ones_like(speed_x)
    heat_x = speed_x * (speed_sq - 2.5)
    heat_y = speed_y * (speed_sq - 2.5)
    heat_z = speed_z * (speed_sq - 2.5)
    moment_rows = (
        jnp.stack(
            [unity, speed_x, speed_y, speed_z, 2.0 / 3.0 * speed_sq - 1.0, heat_x, heat_y, heat_z]
        )
        * weight
    )
    maxwell = jnp.exp(-speed_sq) * math.pi ** (-1.5)
    temp_shape = (speed_sq - 1.5) * maxwell
    shape_rows = jnp.stack(
        [
            maxwell,
            2.0 * speed_x * maxwell,
            2.0 * speed_y * maxwell,
            2.0 * speed_z * maxwell,
            (1.0 - COOLING) * temp_shape,
            SHAKHOV * heat_x * maxwell,
            SHAKHOV * heat_y * maxwell,
            SHAKHOV * heat_z * maxwell,
        ]
    )
    return (speed_x, speed_y, moment_rows, shape_rows, temp_shape)


def wall_moments(moments, wall_flags, wall_temp):
    keep_mask = (jnp.arange(8) == 0).astype(moments.dtype)[:, None, None]
    at_temp = (jnp.arange(8) == 4).astype(moments.dtype)[:, None, None]
    walled = moments * keep_mask + at_temp * wall_temp[None]
    return jnp.where(wall_flags[None] == 1, walled, moments)


def transport(target, padded, speed_x, speed_y, relax_rate):
    along_x = jnp.abs(speed_x)[:, None, None]
    along_y = jnp.abs(speed_y)[:, None, None]
    upwind_x = jnp.where(speed_x[:, None, None] > 0, padded[:, :-2, 1:-1], padded[:, 2:, 1:-1])
    upwind_y = jnp.where(speed_y[:, None, None] > 0, padded[:, 1:-1, :-2], padded[:, 1:-1, 2:])
    return (target * relax_rate + along_x * upwind_x + along_y * upwind_y) / (
        relax_rate + along_x + along_y
    )


def operate(grid_field, diagonal):
    with_rim = with_halo(grid_field, (("space", 0),), 1)
    padded = jnp.pad(with_rim, ((0, 0), (1, 1)))
    beside = padded[2:, 1:-1] + padded[:-2, 1:-1] + padded[1:-1, 2:] + padded[1:-1, :-2]
    return (diagonal + 4.0) * grid_field - beside


def total_one(value):
    return lax.psum(value, "space")


def solve_synthetic(rhs, diagonal):
    solution = jnp.zeros_like(rhs)
    residual = rhs
    direction = rhs
    norm_now = total_one(jnp.sum(residual * residual))
    for rounds in range(ITERS):
        image = operate(direction, diagonal)
        step_size = norm_now / total_one(jnp.sum(direction * image))
        solution = solution + step_size * direction
        residual = residual - step_size * image
        if rounds + 1 < ITERS:
            norm_next = total_one(jnp.sum(residual * residual))
            direction = residual + norm_next / norm_now * direction
            norm_now = norm_next
    return solution


def shards(distribution, vel_index, collision_time, wall_flags, wall_temp):
    slots, rows_x, cols_y = distribution.shape
    highest = lax.Precision.HIGHEST
    speed_x, speed_y, moment_rows, shape_rows, temp_shape = velocity_tables(vel_index)
    flat_dist = distribution.reshape(slots, rows_x * cols_y)
    part_sums = jnp.dot(
        moment_rows, flat_dist, precision=highest, preferred_element_type=jnp.float32
    )
    moments = lax.psum(part_sums, "vel").reshape(8, rows_x, cols_y)
    adjusted = wall_moments(moments, wall_flags, wall_temp)
    target = jnp.dot(
        shape_rows.T,
        adjusted.reshape(8, rows_x * cols_y),
        precision=highest,
        preferred_element_type=jnp.float32,
    ).reshape(slots, rows_x, cols_y)
    with_rim = with_halo(distribution, (("space", 1),), 1)
    padded = jnp.pad(with_rim, ((0, 0), (0, 0), (1, 1)))
    relax_rate = 1.0 / collision_time
    swept = transport(target, padded, speed_x, speed_y, relax_rate)
    temp_part = jnp.dot(
        moment_rows[4:5],
        swept.reshape(slots, rows_x * cols_y),
        precision=highest,
        preferred_element_type=jnp.float32,
    ).reshape(rows_x, cols_y)
    temp_half = lax.psum(temp_part, "vel")
    rhs = temp_half - moments[4]
    diagonal = COOLING / collision_time
    correction = solve_synthetic(rhs, diagonal)
    distribution_new = swept + temp_shape[:, None, None] * correction[None]
    return (distribution_new, correction)


def solution(mesh):
    placed = (
        P("vel", "space", None),
        P("vel"),
        P("space", None),
        P("space", None),
        P("space", None),
    )
    return jax.shard_map(
        shards,
        mesh=mesh,
        in_specs=placed,
        out_specs=(P("vel", "space", None), P("space", None)),
        check_vma=False,
    )
```

profile of v0, /device:TPU:152, one launch (start us, length us, event | category | flops | bytes accessed | tf_op | source)
XLA Modules:
  0.0 943.8 jit_solution(9545877955404522590)
XLA Ops:
  0.6 5.2 copy.7
  5.8 0.0 copy-start.4
  5.9 2.0 fusion.46
  7.9 3.6 collective-permute-start
  11.5 2.3 collective-permute-start.1
  13.7 0.7 add_multiply_fusion
  14.4 0.6 stack.60
  15.0 0.6 stack.61
  15.6 0.7 add_multiply_fusion.1
  16.3 0.6 stack.62
  16.9 0.6 stack.63
  17.5 0.6 stack.64
  18.1 0.6 stack.65
  18.8 0.6 stack.66
  19.4 0.6 stack_broadcast_in_dim.3
  20.0 1.6 stack.67
  21.7 4.2 fusion.1
  25.9 0.6 stack.51
  26.5 0.6 stack.52
  27.1 0.6 stack.53
  27.7 0.6 stack.54
  28.3 0.6 stack.55
  28.9 0.6 stack.56
  29.6 0.6 stack.57
  30.2 0.6 stack.58
  30.8 64.2 %psum.56 = f32[8,256]{1,0:T(8,128)} all-reduce(f32[8,256]{1,0:T(8,128)} %fusion.1), channel_id=1, replica_groups=mesh['vel'=4,'space'=64] {'vel'}, use_global_device_ids=true, to_apply=%region_0.1 | all-reduce | flops 2048 | bytes 16384 | tf_op jit(solution)/shard_map/psum | solution.py:120
  95.0 1.3 slice.126
  96.2 1.6 stack.59
  97.9 0.7 compare_bitcast_fusion
  98.6 0.7 broadcast_divide_fusion
  99.2 0.7 broadcast_compare_fusion
  100.0 0.9 broadcast_multiply_fusion
  100.9 0.0 copy-start.19
  100.9 2.5 select_maximum_fusion
  103.5 6.1 fusion.6
  109.6 1.8 copy-done
  111.4 2.8 fusion.10
  114.2 7.2 psum.57
  121.4 1.9 collective-permute-start.2
  123.3 4.8 collective-permute-start.3
  128.2 1.3 collective-permute-done.3
  129.4 0.1 select_maximum_fusion.6
  129.5 0.7 multiply_reduce_fusion.3
  130.2 158.5 %all-reduce.4 = (f32[]{:T(128)}, f32[]{:T(128)}) all-reduce(f32[]{:T(128)} %get-tuple-element.5, f32[]{:T(128)} %get-tuple-element.4), channel_id=1, replica_groups=mesh['vel'=4,'space'=64] {'space'}, use_global_device_ids=true, to_apply=%region_3.4 | all-reduce | flops 2 | bytes 16 | tf_op jit(solution)/shard_map/psum | solution.py:92
  289.9 0.6 multiply_reduce_fusion.2
  290.5 153.0 %psum.60 = f32[]{:T(128)} all-reduce(f32[]{:T(128)} %get-tuple-element.14), channel_id=1, replica_groups=mesh['vel'=4,'space'=64] {'space'}, use_global_device_ids=true, to_apply=%region_7.8 | all-reduce | flops 1 | bytes 8 | tf_op jit(solution)/shard_map/psum | solution.py:92
  444.8 4.0 collective-permute-start.4
  448.8 2.8 collective-permute-start.5
  451.5 2.7 collective-permute-done.5
  454.2 0.1 select_maximum_fusion.4
  454.3 0.7 multiply_reduce_fusion.1
  455.0 157.0 %psum.61 = f32[]{:T(128)} all-reduce(f32[]{:T(128)} %get-tuple-element.12), channel_id=1, replica_groups=mesh['vel'=4,'space'=64] {'space'}, use_global_device_ids=true, to_apply=%region_9.10 | all-reduce | flops 1 | bytes 8 | tf_op jit(solution)/shard_map/psum | solution.py:92
  613.3 0.6 multiply_reduce_fusion
  613.9 152.8 %psum.62 = f32[]{:T(128)} all-reduce(f32[]{:T(128)} %multiply_reduce_fusion), channel_id=1, replica_groups=mesh['vel'=4,'space'=64] {'space'}, use_global_device_ids=true, to_apply=%region_11.12 | all-reduce | flops 1 | bytes 8 | tf_op jit(solution)/shard_map/psum | solution.py:92
  768.1 3.9 collective-permute-start.6
  772.0 2.8 collective-permute-start.7
  774.8 2.6 collective-permute-done.7
  777.5 0.1 select_maximum_fusion.2
  777.6 0.7 fusion.41
  778.2 157.2 %psum.63 = f32[]{:T(128)} all-reduce(f32[]{:T(128)} %fusion.41), channel_id=1, replica_groups=mesh['vel'=4,'space'=64] {'space'}, use_global_device_ids=true, to_apply=%region_13.14 | all-reduce | flops 1 | bytes 8 | tf_op jit(solution)/shard_map/psum | solution.py:92
  936.7 0.0 copy-start.18
  936.8 0.6 copy-done.18
  937.3 2.3 multiply_add_fusion
  939.7 4.2 copy.12
  (51 shorter events, 0.2 us)
Async XLA Ops:
  5.8 7.9 copy-start.4
  7.9 93.0 %collective-permute-start = (f32[3456,1,128]{0,2,1:T(8,128)}, f32[3456,1,128]{0,2,1:T(8,128)}, u32[]{:S(2)}, u32[]{:S(2)}) collective-permute-start(f32[3456,1,128]{0,2,1:T(8,128)} %get-tuple-element.21), channel_id=1, source_target_pairs={{0,1},{1,2},{2,3},{3,4},{4,5},{5,6},{6,7},{7,8},{8,9},{9,10},{10,1... | collective-permute-start | bytes 5308424 | tf_op jit(solution)/shard_map/ppermute | solution.py:24
  11.5 89.5 %collective-permute-start.1 = (f32[3456,1,128]{0,2,1:T(8,128)}, f32[3456,1,128]{0,2,1:T(8,128)}, u32[]{:S(2)}, u32[]{:S(2)}) collective-permute-start(f32[3456,1,128]{0,2,1:T(8,128)} %get-tuple-element.22), channel_id=1, source_target_pairs={{1,0},{2,1},{3,2},{4,3},{5,4},{6,5},{7,6},{8,7},{9,8},{10,9},{11,1... | collective-permute-start | bytes 5308424 | tf_op jit(solution)/shard_map/ppermute | solution.py:25
  14.4 1.2 copy-start.1
  21.6 4.3 copy-start.12
  21.6 4.9 copy-start.11
  21.6 5.5 copy-start.10
  21.6 6.1 copy-start.9
  21.6 6.7 copy-start.8
  21.6 7.3 copy-start.7
  21.6 7.9 copy-start.6
  21.6 8.5 copy-start.5
  100.9 2.6 copy-start.2
  100.9 2.6 copy-start.13
  100.9 2.6 copy-start.14
  100.9 2.6 copy-start.16
  100.9 2.6 copy-start.19
  109.6 1.8 copy-start
  111.4 10.0 %copy-start.17 = (f32[1,256]{1,0:T(1,128)S(1)}, f32[1,256]{1,0:T(1,128)}, u32[]{:S(2)}) copy-start(f32[1,256]{1,0:T(1,128)} %slice.126) | copy-start | bytes 3076
  111.4 18.1 %copy-start.15 = (f32[2,128]{1,0:T(2,128)S(1)}, f32[2,128]{1,0:T(2,128)}, u32[]{:S(2)}) copy-start(f32[2,128]{1,0:T(2,128)} %param.7) | copy-start | bytes 3076
  111.4 825.9 %copy-start.3 = (f32[3456]{0:T(1024)S(1)}, f32[3456]{0:T(1024)}, u32[]{:S(2)}) copy-start(f32[3456]{0:T(1024)} %get-tuple-element.8) | copy-start | bytes 41476
  121.4 6.8 collective-permute-start.2
  123.3 6.1 collective-permute-start.3
  444.8 6.8 collective-permute-start.4
  448.8 5.5 collective-permute-start.5
  768.1 6.8 collective-permute-start.6
  772.0 5.5 collective-permute-start.7
  936.7 0.6 copy-start.18
where the time goes:
time: 945 us; the launch traced here: 944 us
  blocking collectives  850 us (90%)
  local copies, waits for them, and re-layouts  28.1 us (3%)
  starting transfers between devices  26.1 us (3%)
  matrix products  13.1 us (1%)
  other arithmetic  12.7 us (1%)
    psum x5, blocking collectives, total_one(): return lax.psum(value, 'space')  779 us
    psum x1, blocking collectives, shards(): moments = lax.psum(part_sums, 'vel').reshape(8, rows_x, cols_y)  64.2 us
  transfers between devices with their start and end apart: 8, of which 3 were waited for; matrix products, arithmetic and copies ran while one was open for 2% of the time, Pallas kernels for 0%

commit v1 on v0

v1 whole, which is shorter than its diff:
```python
import functools
import math

import jax
import jax.numpy as jnp
import numpy as np
from jax import lax
from jax.experimental import pallas as pl
from jax.experimental.pallas import tpu as pltpu
from jax.sharding import PartitionSpec as P


VGRID = 24
ITERS = 3
VELOCITY_MAX = 4.5
COOLING = 0.08
SHAKHOV = 0.8 * (1.0 - 2.0 / 3.0)
SPACING = 2.0 * VELOCITY_MAX / VGRID
HIGHEST = lax.Precision.HIGHEST
F32 = jnp.float32
LANES = 128
SLOTS = 3456
HALF = SLOTS // 2
BLOCKS = SLOTS // LANES
PAD = HALF + 8
ROWS = 5
CHUNKS = 9
STEP = BLOCKS // CHUNKS
BF16 = jnp.bfloat16


def class_constants():
    axis = -VELOCITY_MAX + (np.arange(VGRID) + 0.5) * SPACING
    sx, sy, sz = (a.reshape(-1) for a in np.meshgrid(axis, axis, axis, indexing="ij"))
    sq = sx * sx + sy * sy + sz * sz
    maxwell = np.exp(-sq) * math.pi**-1.5
    shapes = np.stack(
        [
            maxwell,
            2.0 * sx * maxwell,
            2.0 * sy * maxwell,
            2.0 * sz * maxwell,
            (1.0 - COOLING) * (sq - 1.5) * maxwell,
            SHAKHOV * sx * (sq - 2.5) * maxwell,
            SHAKHOV * sy * (sq - 2.5) * maxwell,
            SHAKHOV * sz * (sq - 2.5) * maxwell,
        ]
    )
    row = SPACING**3 * (2.0 / 3.0 * sq - 1.0)
    n = np.rint((np.abs(sx) + np.abs(sy)) / SPACING).astype(int)
    table = np.zeros((8, VGRID))
    for m in range(8):
        np.add.at(table[m], n, row * shapes[m])
    return table.astype(np.float32)


def iota(shape, dim):
    return lax.broadcasted_iota(jnp.int32, shape, dim)


def fields(slot_ids):
    v = slot_ids.astype(F32)
    index_x = jnp.floor((v + 0.5) * (1.0 / (VGRID * VGRID)))
    rest = v - index_x * (VGRID * VGRID)
    index_y = jnp.floor((rest + 0.5) * (1.0 / VGRID))
    index_z = rest - index_y * VGRID
    sx = -VELOCITY_MAX + (index_x + 0.5) * SPACING
    sy = -VELOCITY_MAX + (index_y + 0.5) * SPACING
    sz = -VELOCITY_MAX + (index_z + 0.5) * SPACING
    n = jnp.abs(index_x - 11.5) + jnp.abs(index_y - 11.5)
    return sx, sy, sz, sx * sx + sy * sy + sz * sz, n


def prefix(x, size, axis):
    place = iota(x.shape, axis)
    step = 1
    while step < size:
        x = x + jnp.where(place >= step, pltpu.roll(x, step, axis), 0)
        step *= 2
    return x


def spread(x, lane):
    return jnp.broadcast_to(x[:, lane : lane + 1], (8, LANES))


def split(x):
    high = x.astype(BF16)
    return high, (x - high.astype(F32)).astype(BF16)


def fetch(pairs, sem):
    copies = [pltpu.make_async_copy(a, b, sem.at[i]) for i, (a, b) in enumerate(pairs)]
    for copy in copies:
        copy.start()
    return copies


def wait(copies):
    for copy in copies:
        copy.wait()


def pieces(source, target, sem, rows):
    def one(c):
        part = pl.ds(pl.multiple_of(c * STEP * rows, 8), STEP * rows)
        return pltpu.make_async_copy(source.at[part], target.at[part], sem.at[c])

    return one


def compact_kernel(f_hbm, v_hbm, up_hbm, down_hbm, dest_hbm, table_hbm,
                   f_ref, v_ref, square, code_t, dest_t, table, buf_p, buf_n, table_s, sem, f_sem):
    read_v = fetch([(v_hbm, v_ref)], sem)
    piece = pieces(f_hbm, f_ref, f_sem, 2 * LANES)
    for c in range(CHUNKS):
        piece(c).start()
    square[...] = jnp.zeros((LANES, LANES), F32)
    wait(read_v)
    square[0:BLOCKS, :] = jnp.where(v_ref[...] >= VGRID**3 // 2, 1.0, 0.0)
    flags = square[...].T
    row = iota((8, LANES), 0)
    dests, signs = [], []
    for a in range(16):
        sign = flags[8 * a : 8 * a + 8, :].astype(jnp.int32)
        running = prefix(sign, 8, 0)
        count = running[7:8, :]
        table[32 + a : 33 + a, :] = count
        ahead = running - sign
        signs.append(sign)
        dests.append(jnp.where(sign > 0, ahead, count + row - ahead))
    count = table[32:48, :]
    within = prefix(count, 16, 0)
    total = jnp.broadcast_to(within[15:16, :], (16, LANES))
    start = prefix(total, 32, 1) - total + within - count
    place = iota((16, LANES), 0) + 16 * iota((16, LANES), 1)
    table[0:16, :] = start
    table[16:32, :] = HALF - (8 * place - start)
    move = fetch([(table, table_s), (table, table_hbm)], sem)
    for a in range(16):
        dest = dests[a]
        dest_t[8 * a : 8 * a + 8, :] = dest.astype(F32)
        code = 8 * signs[a]
        for j in range(1, 8):
            code = code + jnp.where(jnp.broadcast_to(dest[j : j + 1, :], (8, LANES)) == row, j, 0)
        code_t[8 * a : 8 * a + 8, :] = code
    wait(move)
    keep = fetch([(dest_t, dest_hbm)], sem)

    def step(c, carry):
        piece(c).wait()
        codes = pltpu.roll(code_t[...], LANES - STEP * c, 1)
        for i in range(STEP):
            r = STEP * c + i
            for a in range(16):
                at = 256 * r + 16 * a
                first = f_ref[pl.ds(at, 8, stride=2), :]
                last = f_ref[pl.ds(at + 1, 8, stride=2), :]
                code = spread(codes[8 * a : 8 * a + 8, :], i)
                sent = jnp.where(code >= 8, last, first)
                sent = jnp.take_along_axis(sent, code & 7, axis=0)
                buf_p[pl.ds(table_s[a, r], 8), :] = sent
                buf_n[pl.ds(table_s[16 + a, r], 8), :] = sent
        return carry

    lax.fori_loop(0, CHUNKS, step, 0)
    wait(keep)
    wait(fetch([(buf_p.at[0:HALF], up_hbm), (buf_n.at[8:PAD], down_hbm)], sem))


def shift_lanes(x, by):
    lane = iota(x.shape, 1)
    if by > 0:
        return jnp.where(lane == 0, 0.0, pltpu.roll(x, 1, 1))
    return jnp.where(lane == LANES - 1, 0.0, pltpu.roll(x, LANES - 1, 1))


def dot(a, b):
    return jnp.dot(a, b, precision=HIGHEST, preferred_element_type=F32)


def sums_kernel(f_hbm, v_hbm, tau_hbm, before_hbm, after_hbm, wall_hbm, heat_hbm, c_hbm, payload_hbm, moments_hbm,
                f_ref, v_ref, tau_ref, before_ref, after_ref, wall_ref, heat_ref, c_ref, moments_ref, payload, sem, f_sem):
    read_v = fetch([(v_hbm, v_ref)], sem)
    piece = pieces(f_hbm, f_ref, f_sem, 2 * LANES)
    for c in range(CHUNKS):
        piece(c).start()
    wait(read_v)
    others = fetch([(tau_hbm, tau_ref), (before_hbm, before_ref), (after_hbm, after_ref), (wall_hbm, wall_ref),
                    (heat_hbm, heat_ref), (c_hbm, c_ref)], sem)
    weight = SPACING**3
    classes = iota((VGRID, LANES), 0).astype(F32)

    def step(c, sums):
        piece(c).wait()
        for i in range(STEP):
            r = STEP * c + i
            sx, sy, sz, sq, n = fields(v_ref[pl.ds(r, 1), :])
            row_4 = (2.0 / 3.0 * sq - 1.0) * weight
            heat = (sq - 2.5) * weight
            moments = jnp.concatenate(
                [jnp.full_like(sx, weight), sx * weight, sy * weight, sz * weight, row_4, sx * heat, sy * heat, sz * heat], 0
            )
            hot = classes == n
            parts = [moments]
            for speed in (sx, sy):
                along = row_4 * jnp.abs(speed)
                parts.append(jnp.where(hot, jnp.where(speed > 0, along, 0.0), 0.0))
                parts.append(jnp.where(hot, jnp.where(speed > 0, 0.0, along), 0.0))
            high, low = split(jnp.concatenate(parts, 0))
            both = jnp.concatenate([f_ref[pl.ds(256 * r + x, LANES, stride=2), :] for x in range(2)], 1)
            f_high, f_low = split(both)
            sums = sums + jnp.dot(
                jnp.concatenate([high, high, low], 1), jnp.concatenate([f_high, f_low, f_high], 0),
                preferred_element_type=F32,
            )
        return sums

    sums = lax.fori_loop(0, CHUNKS, step, jnp.zeros((8 + 4 * VGRID, 2 * LANES), F32))
    wait(others)

    def part(x, k):
        return sums[8 + VGRID * k : 8 + VGRID * (k + 1), LANES * x : LANES * (x + 1)]

    def inverse(tau):
        return 1.0 / (1.0 / tau + classes * SPACING)

    where_vel = lax.axis_index("vel")
    lead = jnp.where(where_vel == 0, 1.0, 0.0)
    rows = []
    for x in range(2):
        tau = tau_ref[x : x + 1, :]
        inv = inverse(tau)
        kernels = dot(c_ref[...], inv) * (1.0 / tau)
        moments = sums[0:8, LANES * x : LANES * (x + 1)]
        product = moments * kernels
        gas = jnp.sum(product, 0, keepdims=True)
        wall = product[0:1, :] + lead * heat_ref[x : x + 1, :] * kernels[4:5, :]
        held = jnp.where(wall_ref[x : x + 1, :] == 1, wall, gas) - moments[4:5, :]
        across = part(1, 1) if x == 0 else part(0, 0)
        moved = inv * (across + shift_lanes(part(x, 2), 1) + shift_lanes(part(x, 3), -1))
        moments_ref[8 * x : 8 * x + 8, :] = moments
        rows.append(held + jnp.sum(moved, 0, keepdims=True))
    rows.append(jnp.sum(inverse(before_ref[...]) * part(0, 1), 0, keepdims=True))
    rows.append(jnp.sum(inverse(after_ref[...]) * part(1, 0), 0, keepdims=True))
    rows.append(jnp.where(where_vel == 0, tau_ref[0:1, :], tau_ref[1:2, :]))
    for k in range(8):
        for j in range(ROWS):
            payload[ROWS * k + j : ROWS * k + j + 1, :] = rows[j]
    block = payload[0 : 8 * ROWS, :]
    for k in range(1, 32):
        payload[8 * ROWS * k : 8 * ROWS * (k + 1), :] = block
    wait(fetch([(moments_ref, moments_hbm), (payload, payload_hbm)], sem))


def sweep_kernel(f_hbm, v_hbm, mine_hbm, other_hbm, tau_hbm, wall_hbm, heat_hbm, dest_hbm, pre_hbm, along_hbm, shape_hbm, index_hbm,
                 f_ref, v_ref, mine_ref, other_ref, tau_ref, wall_ref, heat_ref, dest_ref, pre_ref, along_ref, shape_ref, index_ref,
                 rhs, cols, sem, f_sem, pre_sem, along_sem, shape_sem, index_sem):
    first = fetch([(v_hbm, v_ref), (mine_hbm, mine_ref), (other_hbm, other_ref), (tau_hbm, tau_ref), (wall_hbm, wall_ref),
                   (heat_hbm, heat_ref), (dest_hbm, dest_ref)], sem)
    piece = pieces(f_hbm, f_ref, f_sem, 2 * LANES)
    for c in range(CHUNKS):
        piece(c).start()
    outs = [pieces(pre_ref, pre_hbm, pre_sem, 2 * LANES), pieces(along_ref, along_hbm, along_sem, LANES),
            pieces(shape_ref, shape_hbm, shape_sem, LANES), pieces(index_ref, index_hbm, index_sem, LANES)]
    rhs[...] = jnp.zeros((LANES, 8 * LANES), F32)
    cols[...] = jnp.zeros((LANES, LANES), F32)
    row = iota((8, LANES), 0)
    classes = iota((VGRID, LANES), 0).astype(F32)
    wait(first)
    dest_ref[...] = dest_ref[...].T
    for x in range(2):
        moments = mine_ref[8 * x : 8 * x + 8, :] + other_ref[8 * x : 8 * x + 8, :]
        wall = jnp.where(row == 0, moments, jnp.where(row == 4, heat_ref[x : x + 1, :], 0.0))
        relax = 1.0 / tau_ref[x : x + 1, :]
        adjusted = jnp.where(wall_ref[x : x + 1, :] == 1, wall, moments)
        high, low = (p.astype(F32) for p in split(adjusted * relax))
        here = slice(LANES * x, LANES * (x + 1))
        rhs[0:8, here] = high
        rhs[8:16, here] = low
        rhs[16:24, here] = high
        high, low = (p.astype(F32) for p in split(1.0 / (relax + classes * SPACING)))
        here = slice(LANES * (2 + x), LANES * (3 + x))
        rhs[24:48, here] = high
        rhs[48:72, here] = low
    for k, rows in enumerate(((0,), (1,), (2, 3), (4,))):
        mask = functools.reduce(jnp.logical_or, [row == j for j in rows])
        rhs[72:80, LANES * (4 + k) : LANES * (5 + k)] = jnp.where(mask, 1.0, 0.0)
    rhs_value = rhs[...].astype(BF16)

    def step(c, carry):
        piece(c).wait()
        for i in range(STEP):
            r = STEP * c + i
            sx, sy, sz, sq, n = fields(v_ref[pl.ds(r, 1), :])
            maxwell = jnp.exp(-sq) * math.pi**-1.5
            shape = (sq - 1.5) * maxwell
            heat = SHAKHOV * (sq - 2.5) * maxwell
            high, low = (p.astype(F32) for p in split(jnp.concatenate(
                [maxwell, 2.0 * sx * maxwell, 2.0 * sy * maxwell, 2.0 * sz * maxwell,
                 (1.0 - COOLING) * shape, sx * heat, sy * heat, sz * heat], 0)))
            shape_high, shape_low = (p.astype(F32) for p in split(shape))
            hot = jnp.where(classes == n, 1.0, 0.0)
            zero = jnp.zeros_like(sx)
            cols[0:80, :] = jnp.concatenate(
                [high, high, low, hot, hot, sx, sy, shape_high, shape_low, dest_ref[pl.ds(r, 1), :], zero, zero, zero], 0)
            made = jnp.dot(cols[...].T.astype(BF16), rhs_value, preferred_element_type=F32)
            speed_x, speed_y = made[:, 4 * LANES : 5 * LANES], made[:, 5 * LANES : 6 * LANES]
            rows = [f_ref[pl.ds(256 * r + x, LANES, stride=2), :] for x in range(2)]
            along_x, along_y = jnp.abs(speed_x), jnp.abs(speed_y)
            ahead = speed_x > 0
            for x in range(2):
                upwind_y = jnp.where(speed_y > 0, shift_lanes(rows[x], 1), shift_lanes(rows[x], -1))
                near = jnp.where(ahead, 0.0, rows[1]) if x == 0 else jnp.where(ahead, rows[0], 0.0)
                inv = made[:, LANES * (2 + x) : LANES * (3 + x)]
                value = (made[:, LANES * x : LANES * (x + 1)] + along_x * near + along_y * upwind_y) * inv
                pre_ref[pl.ds(256 * r + x, LANES, stride=2), :] = value
            at = pl.ds(pl.multiple_of(LANES * r, LANES), LANES)
            along_ref[at, :] = speed_x * jnp.where(ahead, made[:, 2 * LANES : 3 * LANES], made[:, 3 * LANES : 4 * LANES])
            shape_ref[at, :] = made[:, 6 * LANES : 7 * LANES]
            index_ref[at, :] = made[:, 7 * LANES :].astype(jnp.int32)
        for out in outs:
            out(c).start()
        return carry

    lax.fori_loop(0, CHUNKS, step, 0)
    for c in range(CHUNKS):
        for out in outs:
            out(c).wait()


def solve_kernel(y_hbm, out_ref, y_ref, kept, sem):
    wait(fetch([(y_hbm, y_ref)], sem))

    def take(device, j):
        return y_ref[pl.ds(ROWS * device + j, 64, stride=ROWS), :]

    place = iota((64, LANES), 0)

    def lower(x):
        return jnp.where(place == 0, 0.0, pltpu.roll(x, 1, 0))

    def upper(x):
        return jnp.where(place == 63, 0.0, pltpu.roll(x, 63, 0))

    def over_vel(j):
        return take(0, j) + take(64, j) + take(128, j) + take(192, j)

    even = over_vel(0) + lower(over_vel(3))
    odd = over_vel(1) + upper(over_vel(2))
    middle_even = COOLING / take(0, 4) + 4.0
    middle_odd = COOLING / take(64, 4) + 4.0

    def operate(e, o):
        image_e = middle_even * e - (lower(o) + o + shift_lanes(e, 1) + shift_lanes(e, -1))
        image_o = middle_odd * o - (e + upper(e) + shift_lanes(o, 1) + shift_lanes(o, -1))
        return image_e, image_o

    def inner(a, b):
        total = jnp.sum(a[0] * b[0] + a[1] * b[1], 0, keepdims=True)
        return jnp.sum(total, 1, keepdims=True)

    residual = (even, odd)
    direction = residual
    found = (jnp.zeros_like(even), jnp.zeros_like(odd))
    norm_now = inner(residual, residual)
    for rounds in range(ITERS):
        image = operate(*direction)
        step_size = norm_now / inner(direction, image)
        found = tuple(v + step_size * d for v, d in zip(found, direction))
        if rounds + 1 < ITERS:
            residual = tuple(r - step_size * i for r, i in zip(residual, image))
            norm_next = inner(residual, residual)
            direction = tuple(r + norm_next / norm_now * d for r, d in zip(residual, direction))
            norm_now = norm_next
    kept[0:64, :] = found[0]
    kept[64:128, :] = found[1]
    out_ref[0:1, :] = kept[pl.ds(lax.axis_index("space"), 1), :]
    out_ref[1:2, :] = kept[pl.ds(64 + lax.axis_index("space"), 1), :]


def finish_kernel(pre_hbm, along_hbm, shape_hbm, index_hbm, corr_hbm, up_hbm, down_hbm, table_hbm, out_hbm,
                  pre_ref, along_ref, shape_ref, index_ref, corr_ref, buf_p, buf_n, table_s, out_ref,
                  sem, pre_sem, along_sem, shape_sem, index_sem, out_sem):
    first = fetch([(table_hbm, table_s), (corr_hbm, corr_ref), (up_hbm, buf_p.at[0:HALF]), (down_hbm, buf_n.at[8:PAD])], sem)
    ins = [pieces(pre_hbm, pre_ref, pre_sem, 2 * LANES), pieces(along_hbm, along_ref, along_sem, LANES),
           pieces(shape_hbm, shape_ref, shape_sem, LANES), pieces(index_hbm, index_ref, index_sem, LANES)]
    done = pieces(out_ref, out_hbm, out_sem, 2 * LANES)
    for c in range(CHUNKS):
        for piece in ins:
            piece(c).start()
    wait(first)
    corr = [jnp.broadcast_to(corr_ref[x : x + 1, :], (8, LANES)) for x in range(2)]
    row = iota((8, LANES), 0)

    def step(c, carry):
        for piece in ins:
            piece(c).wait()
        for i in range(STEP):
            r = STEP * c + i
            for a in range(16):
                at = 128 * r + 8 * a
                here = pl.ds(pl.multiple_of(at, 8), 8)
                halo = jnp.where(row < table_s[32 + a, r], buf_p[pl.ds(table_s[a, r], 8), :],
                                 buf_n[pl.ds(table_s[16 + a, r], 8), :])
                moved = along_ref[here, :] * jnp.take_along_axis(halo, index_ref[here, :], axis=0)
                ahead = along_ref[here, :] > 0
                shape = shape_ref[here, :]
                near = pl.ds(2 * at, 8, stride=2)
                far = pl.ds(2 * at + 1, 8, stride=2)
                out_ref[near, :] = pre_ref[near, :] + jnp.where(ahead, moved, 0.0) + shape * corr[0]
                out_ref[far, :] = pre_ref[far, :] - jnp.where(ahead, 0.0, moved) + shape * corr[1]
        done(c).start()
        return carry

    lax.fori_loop(0, CHUNKS, step, 0)
    for c in range(CHUNKS):
        done(c).wait()


def vmem(shape, dtype=F32):
    return pltpu.VMEM(shape, dtype)


def struct(shape, dtype=F32):
    return jax.ShapeDtypeStruct(shape, dtype)


IN_HBM = pl.BlockSpec(memory_space=pl.ANY)
IN_VMEM = pl.BlockSpec(memory_space=pltpu.VMEM)
DMA = pltpu.SemaphoreType.DMA
INT = jnp.int32


def call(kernel, outs, scratch, args, flops, out_spec=IN_HBM):
    return pl.pallas_call(
        kernel,
        out_shape=outs,
        in_specs=[IN_HBM] * len(args),
        out_specs=jax.tree.map(lambda _: out_spec, outs),
        scratch_shapes=scratch,
        cost_estimate=pl.CostEstimate(flops=flops, bytes_accessed=8 << 20, transcendentals=0),
    )(*args)


def program(distribution, vel_index, collision_time, wall_flags, wall_temp):
    space = lax.axis_size("space")
    vel = lax.axis_size("vel")
    up = [(i, i + 1) for i in range(space - 1)]
    down = [(j, i) for i, j in up]
    partner = [(i, i ^ 1) for i in range(vel)]
    opposite = [(i, (i + vel // 2) % vel) for i in range(vel)]

    flat = distribution.reshape(2 * SLOTS, LANES)
    ids = vel_index.reshape(BLOCKS, LANES)
    small, square, whole, halves = (2, LANES), (LANES, LANES), (2 * SLOTS, LANES), (SLOTS, LANES)
    before = lax.ppermute(collision_time[1:2], "space", up)
    after = lax.ppermute(collision_time[0:1], "space", down)
    rows_up, rows_down, dest, table = call(
        compact_kernel,
        (struct((HALF, LANES)), struct((HALF, LANES)), struct(square), struct((48, LANES), INT)),
        [vmem(whole), vmem((BLOCKS, LANES), INT), vmem(square), vmem(square, INT), vmem(square), vmem((48, LANES), INT),
         vmem((PAD, LANES)), vmem((PAD, LANES)), pltpu.SMEM((48, LANES), INT), DMA((2,)), DMA((CHUNKS,))],
        (flat, ids), 1 << 20,
    )
    halo_up = lax.ppermute(rows_up, "space", up)
    payload, moments = call(
        sums_kernel, (struct((ROWS * vel * space, LANES)), struct((16, LANES))),
        [vmem(whole), vmem((BLOCKS, LANES), INT), vmem(small), vmem((1, LANES)), vmem((1, LANES)), vmem(small, INT), vmem(small),
         vmem((8, VGRID)), vmem((16, LANES)), vmem((256 * ROWS, LANES)), DMA((6,)), DMA((CHUNKS,))],
        (flat, ids, collision_time, before, after, wall_flags, wall_temp, jnp.asarray(class_constants())), 1 << 30,
    )
    gathered = lax.all_to_all(payload.reshape(vel * space, 1, ROWS * LANES), ("vel", "space"), 0, 0, tiled=True)
    moments = moments + lax.ppermute(moments, "vel", partner)
    moments_other = lax.ppermute(moments, "vel", opposite)
    halo_down = lax.ppermute(rows_down, "space", down)
    pre, along, shape, index = call(
        sweep_kernel,
        (struct(whole), struct(halves), struct(halves), struct(halves, INT)),
        [vmem(whole), vmem((BLOCKS, LANES), INT), vmem((16, LANES)), vmem((16, LANES)), vmem(small), vmem(small, INT), vmem(small),
         vmem(square), vmem(whole), vmem(halves), vmem(halves), vmem(halves, INT), vmem((LANES, 8 * LANES)), vmem(square),
         DMA((7,)), DMA((CHUNKS,)), DMA((CHUNKS,)), DMA((CHUNKS,)), DMA((CHUNKS,)), DMA((CHUNKS,))],
        (flat, ids, moments, moments_other, collision_time, wall_flags, wall_temp, dest), 1 << 30,
    )
    correction = call(
        solve_kernel, struct(small), [vmem((ROWS * vel * space, LANES)), vmem(square), DMA((1,))],
        (gathered.reshape(ROWS * vel * space, LANES),), 1 << 24, IN_VMEM,
    )
    result = call(
        finish_kernel, struct(whole),
        [vmem(whole), vmem(halves), vmem(halves), vmem(halves, INT), vmem(small), vmem((PAD, LANES)), vmem((PAD, LANES)),
         pltpu.SMEM((48, LANES), INT), vmem(whole), DMA((4,))] + [DMA((CHUNKS,))] * 5,
        (pre, along, shape, index, correction, halo_up, halo_down, table), 1 << 24,
    )
    return result.reshape(SLOTS, 2, LANES), correction


def solution(mesh):
    placed = (
        P("vel", "space", None),
        P("vel"),
        P("space", None),
        P("space", None),
        P("space", None),
    )
    return jax.shard_map(
        program,
        mesh=mesh,
        in_specs=placed,
        out_specs=(P("vel", "space", None), P("space", None)),
        check_vma=False,
    )
```

time: 945 us -> 110 us (0.12)
  the two profiles are of different devices: /device:TPU:152 before, /device:TPU:1 now
where the time goes in v1:
time: 110 us; the launch traced here: 109 us
  waiting for transfers between devices  40.6 us (37%)
  starting transfers between devices  34.9 us (32%)
  Pallas kernels  28.9 us (26%)
  local copies, waits for them, and re-layouts  3.92 us (4%)
    ppermute x1, waiting for transfers between devices, program(): moments_other = lax.ppermute(moments, 'vel', opposite)  39.1 us
    pallas_call x5, Pallas kernels, call(): pl.pallas_call(kernel, out_shape=outs, in_specs=[IN_HBM] * len(args), out...  28.9 us
    all_to_all x1, starting transfers between devices, program(): lax.all_to_all(payload.reshape(vel * space, 1, ROWS * LANES), ('vel', 'sp...  21.2 us
    ppermute x1, starting transfers between devices, program(): before = lax.ppermute(collision_time[1:2], 'space', up)  4.65 us
    ppermute x1, starting transfers between devices, program(): halo_up = lax.ppermute(rows_up, 'space', up)  3.31 us
    unnamed x16, local copies, waits for them, and re-layouts  3.16 us
    ppermute x1, starting transfers between devices, program(): moments_other = lax.ppermute(moments, 'vel', opposite)  2.44 us
  transfers between devices with their start and end apart: 7, of which 3 were waited for; matrix products, arithmetic and copies ran while one was open for 0% of the time, Pallas kernels for 15%

profile of v1, /device:TPU:1, one launch (start us, length us, event | category | flops | bytes accessed | tf_op | source)
XLA Modules:
  0.0 109.2 jit_solution(14998007956255589241)
XLA Ops:
  0.6 0.8 fusion
  1.4 1.3 %collective-permute-start.1 = (f32[1,128]{1,0:T(1,128)S(1)}, f32[1,128]{1,0:T(1,128)S(1)}, u32[]{:S(2)}, u32[]{:S(2)}) collective-permute-start(f32[1,128]{1,0:T(1,128)S(1)} %get-tuple-element.22), channel_id=1, source_target_pairs={{1,0},{2,1},{3,2},{4,3},{5,4},{6,5},{7,6},{8,7},{9,8},{10,9},{11,1... | collective-permute-start | bytes 1544 | tf_op jit(solution)/shard_map/ppermute | solution.py:458
  2.7 4.6 %collective-permute-start = (f32[1,128]{1,0:T(1,128)S(1)}, f32[1,128]{1,0:T(1,128)S(1)}, u32[]{:S(2)}, u32[]{:S(2)}) collective-permute-start(f32[1,128]{1,0:T(1,128)S(1)} %get-tuple-element.23), channel_id=1, source_target_pairs={{0,1},{1,2},{2,3},{3,4},{4,5},{5,6},{6,7},{7,8},{8,9},{9,10},{10,1... | collective-permute-start | bytes 1544 | tf_op jit(solution)/shard_map/ppermute | solution.py:457
  7.3 0.0 collective-permute-done.1.after_hbm
  7.3 0.0 copy-start.6
  7.4 0.7 collective-permute-done.before_hbm
  8.0 0.0 copy-start.7
  8.0 0.0 copy-done.6
  8.0 0.5 copy-done.7
  8.5 5.4 %shard_map.77 = (f32[1280,128]{1,0:T(8,128)}, f32[16,128]{1,0:T(8,128)}) custom-call(f32[6912,128]{1,0:T(8,128)} %bitcast.5, s32[27,128]{1,0:T(8,128)} %bitcast.11, f32[2,128]{1,0:T(2,128)} %tau_hbm.3, f32[1,128]{1,0:T(1,128)} %copy-done.7, f32[1,128]{1,0:T(1,128)} %copy-done.6, s32[2,128]{1,0:T(2,128)} %wall_hbm.3, f32[2,128]{1,0:T(2,128)} %heat_hbm.3, ...), custom_call_target="tpu_custom_call" | custom-call | flops 1073741824 | bytes 8388608 | tf_op jit(solution)/shard_map/pallas_call | solution.py:436
  14.0 0.0 copy-start.3
  14.0 21.2 %all-to-all-start = ((f32[256,1,640]{2,1,0:T(1,128)}), f32[256,1,640]{2,1,0:T(1,128)S(1)}, u32[]{:S(2)}, u32[]{:S(2)}) async-start(f32[256,1,640]{2,1,0:T(1,128)} %bitcast.10), calls=%async_computation | async-start | bytes 1310720 | tf_op jit(solution)/shard_map/all_to_all | solution.py:473
  35.2 6.7 %shard_map.78 = (f32[1728,128]{1,0:T(8,128)}, f32[1728,128]{1,0:T(8,128)}, f32[128,128]{1,0:T(8,128)}, s32[48,128]{1,0:T(8,128)}) custom-call(f32[6912,128]{1,0:T(8,128)} %bitcast.6, s32[27,128]{1,0:T(8,128)} %bitcast.12), custom_call_target="tpu_custom_call" | custom-call | flops 1048576 | bytes 8388608 | tf_op jit(solution)/shard_map/pallas_call | solution.py:436
  41.8 3.3 %collective-permute-start.4 = (f32[1728,128]{1,0:T(8,128)}, f32[1728,128]{1,0:T(8,128)S(1)}, u32[]{:S(2)}, u32[]{:S(2)}) collective-permute-start(f32[1728,128]{1,0:T(8,128)} %get-tuple-element.19), channel_id=1, source_target_pairs={{0,1},{1,2},{2,3},{3,4},{4,5},{5,6},{6,7},{7,8},{8,9},{9,10},{10,1... | collective-permute-start | bytes 2654216 | tf_op jit(solution)/shard_map/ppermute | solution.py:466
  45.2 1.3 %collective-permute-start.5 = (f32[1728,128]{1,0:T(8,128)}, f32[1728,128]{1,0:T(8,128)S(1)}, u32[]{:S(2)}, u32[]{:S(2)}) collective-permute-start(f32[1728,128]{1,0:T(8,128)} %get-tuple-element.20), channel_id=1, source_target_pairs={{1,0},{2,1},{3,2},{4,3},{5,4},{6,5},{7,6},{8,7},{9,8},{10,9},{11,1... | collective-permute-start | bytes 2654216 | tf_op jit(solution)/shard_map/ppermute | solution.py:476
  46.5 0.0 copy-done.3
  46.5 0.8 collective-permute-start.2
  47.2 0.8 collective-permute-done.2
  48.1 0.0 copy-start.4
  48.1 2.4 %collective-permute-start.3 = (f32[16,128]{1,0:T(8,128)S(1)}, f32[16,128]{1,0:T(8,128)S(1)}, u32[]{:S(2)}, u32[]{:S(2)}) collective-permute-start(f32[16,128]{1,0:T(8,128)S(1)} %add.3.mine_hbm), channel_id=1, source_target_pairs={{0,128},{64,192},{128,0},{192,64},{1,129},{65,193},{129,1},{193,65... | collective-permute-start | bytes 24584 | tf_op jit(solution)/shard_map/ppermute | solution.py:475
  50.5 39.1 %collective-permute-done.3.other_hbm = f32[16,128]{1,0:T(8,128)S(1)} collective-permute-done((f32[16,128]{1,0:T(8,128)S(1)}, f32[16,128]{1,0:T(8,128)S(1)}, u32[]{:S(2)}, u32[]{:S(2)}) %collective-permute-start.3) | collective-permute-done | bytes 8224 | tf_op jit(solution)/shard_map/ppermute | solution.py:475
  89.6 0.0 copy-start.5
  89.6 0.0 copy-done.4
  89.6 0.6 copy-done.5
  90.2 7.8 %shard_map.79 = (f32[6912,128]{1,0:T(8,128)}, f32[3456,128]{1,0:T(8,128)}, f32[3456,128]{1,0:T(8,128)}, s32[3456,128]{1,0:T(8,128)}) custom-call(f32[6912,128]{1,0:T(8,128)} %bitcast.7, s32[27,128]{1,0:T(8,128)} %bitcast.13, f32[16,128]{1,0:T(8,128)} %copy-done.4, f32[16,128]{1,0:T(8,128)} %copy-done.5, f32[2,128]{1,0:T(2,128)} %tau_hbm.3, ...), custom_call_target="tpu_custom_call" | custom-call | flops 1073741824 | bytes 8388608 | tf_op jit(solution)/shard_map/pallas_call | solution.py:436
  98.0 0.0 all-to-all-done
  98.0 0.0 copy-start
  98.0 0.8 copy-done
  98.9 2.5 %shard_map.80.corr_hbm = f32[2,128]{1,0:T(2,128)} custom-call(f32[1280,128]{1,0:T(8,128)} %bitcast.9), custom_call_target="tpu_custom_call" | custom-call | flops 16777216 | bytes 8388608 | tf_op jit(solution)/shard_map/pallas_call | solution.py:436
  101.3 0.0 collective-permute-done.4.up_hbm
  101.3 0.0 copy-start.1
  101.4 0.0 collective-permute-done.5.down_hbm
  101.4 0.0 copy-start.2
  101.4 0.9 copy-done.1
  102.3 0.3 copy-done.2
  102.6 6.6 %shard_map.81 = f32[6912,128]{1,0:T(8,128)} custom-call(f32[6912,128]{1,0:T(8,128)} %get-tuple-element.14.pre_hbm, f32[3456,128]{1,0:T(8,128)} %get-tuple-element.15.along_hbm, f32[3456,128]{1,0:T(8,128)} %get-tuple-element.16.shape_hbm, s32[3456,128]{1,0:T(8,128)} %get-tuple-element.17.index_hbm, f32[2,128]{1,0:T(2,128)} %shard_map.80.corr_hbm, ...), custom_call_target="tpu_custom_call" | custom-call | flops 16777216 | bytes 8388608 | tf_op jit(solution)/shard_map/pallas_call | solution.py:436
  (1 shorter events, 0.0 us)
Async XLA Ops:
  1.4 5.9 %collective-permute-start.1 = (f32[1,128]{1,0:T(1,128)S(1)}, f32[1,128]{1,0:T(1,128)S(1)}, u32[]{:S(2)}, u32[]{:S(2)}) collective-permute-start(f32[1,128]{1,0:T(1,128)S(1)} %get-tuple-element.22), channel_id=1, source_target_pairs={{1,0},{2,1},{3,2},{4,3},{5,4},{6,5},{7,6},{8,7},{9,8},{10,9},{11,1... | collective-permute-start | bytes 1544 | tf_op jit(solution)/shard_map/ppermute | solution.py:458
  2.7 5.4 %collective-permute-start = (f32[1,128]{1,0:T(1,128)S(1)}, f32[1,128]{1,0:T(1,128)S(1)}, u32[]{:S(2)}, u32[]{:S(2)}) collective-permute-start(f32[1,128]{1,0:T(1,128)S(1)} %get-tuple-element.23), channel_id=1, source_target_pairs={{0,1},{1,2},{2,3},{3,4},{4,5},{5,6},{6,7},{7,8},{8,9},{9,10},{10,1... | collective-permute-start | bytes 1544 | tf_op jit(solution)/shard_map/ppermute | solution.py:457
  7.3 0.7 copy-start.6
  8.0 0.5 copy-start.7
  14.0 32.5 %copy-start.3 = (f32[16,128]{1,0:T(8,128)S(1)}, f32[16,128]{1,0:T(8,128)}, u32[]{:S(2)}) copy-start(f32[16,128]{1,0:T(8,128)} %get-tuple-element.12) | copy-start | bytes 24580
  14.0 84.0 %all-to-all-start = ((f32[256,1,640]{2,1,0:T(1,128)}), f32[256,1,640]{2,1,0:T(1,128)S(1)}, u32[]{:S(2)}, u32[]{:S(2)}) async-start(f32[256,1,640]{2,1,0:T(1,128)} %bitcast.10), calls=%async_computation | async-start | bytes 1310720 | tf_op jit(solution)/shard_map/all_to_all | solution.py:473
  41.8 59.5 %collective-permute-start.4 = (f32[1728,128]{1,0:T(8,128)}, f32[1728,128]{1,0:T(8,128)S(1)}, u32[]{:S(2)}, u32[]{:S(2)}) collective-permute-start(f32[1728,128]{1,0:T(8,128)} %get-tuple-element.19), channel_id=1, source_target_pairs={{0,1},{1,2},{2,3},{3,4},{4,5},{5,6},{6,7},{7,8},{8,9},{9,10},{10,1... | collective-permute-start | bytes 2654216 | tf_op jit(solution)/shard_map/ppermute | solution.py:466
  45.2 56.2 %collective-permute-start.5 = (f32[1728,128]{1,0:T(8,128)}, f32[1728,128]{1,0:T(8,128)S(1)}, u32[]{:S(2)}, u32[]{:S(2)}) collective-permute-start(f32[1728,128]{1,0:T(8,128)} %get-tuple-element.20), channel_id=1, source_target_pairs={{1,0},{2,1},{3,2},{4,3},{5,4},{6,5},{7,6},{8,7},{9,8},{10,9},{11,1... | collective-permute-start | bytes 2654216 | tf_op jit(solution)/shard_map/ppermute | solution.py:476
  46.5 1.6 %collective-permute-start.2 = (f32[16,128]{1,0:T(8,128)S(1)}, f32[16,128]{1,0:T(8,128)S(1)}, u32[]{:S(2)}, u32[]{:S(2)}) collective-permute-start(f32[16,128]{1,0:T(8,128)S(1)} %copy-done.3), channel_id=1, source_target_pairs={{0,64},{64,0},{128,192},{192,128},{1,65},{65,1},{129,193},{193,129... | collective-permute-start | bytes 24584 | tf_op jit(solution)/shard_map/ppermute | solution.py:474
  48.1 41.6 %copy-start.4 = (f32[16,128]{1,0:T(8,128)}, f32[16,128]{1,0:T(8,128)S(1)}, u32[]{:S(2)}) copy-start(f32[16,128]{1,0:T(8,128)S(1)} %add.3.mine_hbm) | copy-start | bytes 24580
  48.1 41.6 %collective-permute-start.3 = (f32[16,128]{1,0:T(8,128)S(1)}, f32[16,128]{1,0:T(8,128)S(1)}, u32[]{:S(2)}, u32[]{:S(2)}) collective-permute-start(f32[16,128]{1,0:T(8,128)S(1)} %add.3.mine_hbm), channel_id=1, source_target_pairs={{0,128},{64,192},{128,0},{192,64},{1,129},{65,193},{129,1},{193,65... | collective-permute-start | bytes 24584 | tf_op jit(solution)/shard_map/ppermute | solution.py:475
  89.6 0.6 copy-start.5
  98.0 0.8 copy-start
  101.3 0.9 copy-start.1
  101.4 1.2 %copy-start.2 = (f32[1728,128]{1,0:T(8,128)}, f32[1728,128]{1,0:T(8,128)S(1)}, u32[]{:S(2)}) copy-start(f32[1728,128]{1,0:T(8,128)S(1)} %collective-permute-done.5.down_hbm) | copy-start | bytes 2654212

commit v2 on v1

v2 whole, which is shorter than its diff:
```python
import math

import jax
import jax.numpy as jnp
import numpy as np
from jax import lax
from jax.experimental import pallas as pl
from jax.experimental.pallas import tpu as pltpu
from jax.sharding import PartitionSpec as P


VGRID = 24
ITERS = 3
VELOCITY_MAX = 4.5
COOLING = 0.08
SHAKHOV = 0.8 * (1.0 - 2.0 / 3.0)
SPACING = 2.0 * VELOCITY_MAX / VGRID
HIGHEST = lax.Precision.HIGHEST
F32 = jnp.float32
LANES = 128
SLOTS = 3456
HALF = SLOTS // 2
BLOCKS = SLOTS // LANES
PAD = HALF + 8
ROWS = 6
EARLY = 1000
CHUNKS = 9
STEP = BLOCKS // CHUNKS
BF16 = jnp.bfloat16


def class_constants():
    axis = -VELOCITY_MAX + (np.arange(VGRID) + 0.5) * SPACING
    sx, sy, sz = (a.reshape(-1) for a in np.meshgrid(axis, axis, axis, indexing="ij"))
    sq = sx * sx + sy * sy + sz * sz
    maxwell = np.exp(-sq) * math.pi**-1.5
    shapes = np.stack(
        [
            maxwell,
            2.0 * sx * maxwell,
            2.0 * sy * maxwell,
            2.0 * sz * maxwell,
            (1.0 - COOLING) * (sq - 1.5) * maxwell,
            SHAKHOV * sx * (sq - 2.5) * maxwell,
            SHAKHOV * sy * (sq - 2.5) * maxwell,
            SHAKHOV * sz * (sq - 2.5) * maxwell,
        ]
    )
    row = SPACING**3 * (2.0 / 3.0 * sq - 1.0)
    n = np.rint((np.abs(sx) + np.abs(sy)) / SPACING).astype(int)
    table = np.zeros((8, VGRID))
    for m in range(8):
        np.add.at(table[m], n, row * shapes[m])
    return table.astype(np.float32)


def iota(shape, dim):
    return lax.broadcasted_iota(jnp.int32, shape, dim)


def fields(slot_ids):
    v = slot_ids.astype(F32)
    index_x = jnp.floor((v + 0.5) * (1.0 / (VGRID * VGRID)))
    rest = v - index_x * (VGRID * VGRID)
    index_y = jnp.floor((rest + 0.5) * (1.0 / VGRID))
    index_z = rest - index_y * VGRID
    sx = -VELOCITY_MAX + (index_x + 0.5) * SPACING
    sy = -VELOCITY_MAX + (index_y + 0.5) * SPACING
    sz = -VELOCITY_MAX + (index_z + 0.5) * SPACING
    n = jnp.abs(index_x - 11.5) + jnp.abs(index_y - 11.5)
    return sx, sy, sz, sx * sx + sy * sy + sz * sz, n


def spread(x, lane):
    return jnp.broadcast_to(x[:, lane : lane + 1], (8, LANES))


def split(x):
    high = x.astype(BF16)
    return high, (x - high.astype(F32)).astype(BF16)


def fetch(pairs, sem):
    copies = [pltpu.make_async_copy(a, b, sem.at[i]) for i, (a, b) in enumerate(pairs)]
    for copy in copies:
        copy.start()
    return copies


def wait(copies):
    for copy in copies:
        copy.wait()


def pieces(source, target, sem, rows):
    def one(c):
        part = pl.ds(pl.multiple_of(c * STEP * rows, 8), STEP * rows)
        return pltpu.make_async_copy(source.at[part], target.at[part], sem.at[c])

    return one


def compact_kernel(f_hbm, v_hbm, up_hbm, early_hbm, late_hbm, dest_hbm, table_hbm,
                   f_ref, v_ref, square, code_t, dest_t, table, buf_p, buf_n, table_s, sem, f_sem):
    read_v = fetch([(v_hbm, v_ref)], sem)
    piece = pieces(f_hbm, f_ref, f_sem, 2 * LANES)
    for c in range(CHUNKS):
        piece(c).start()
    square[...] = jnp.zeros((LANES, LANES), F32)
    down, along = iota((LANES, LANES), 0), iota((LANES, LANES), 1)
    inside = jnp.where((down // 8 == along // 8) & (along < down), 1.0, 0.0).astype(BF16)
    group = iota((16, LANES), 0)
    before = jnp.where(iota((16, LANES), 1) // 8 < group, 1.0, 0.0).astype(BF16)
    within = jnp.where(iota((16, LANES), 1) // 8 == group, 1.0, 0.0).astype(BF16)
    earlier = jnp.where(down < along, 1.0, 0.0).astype(BF16)
    wait(read_v)
    square[0:BLOCKS, :] = jnp.where(v_ref[...] >= VGRID**3 // 2, 1.0, 0.0)
    flags = square[...].T

    def count_of(a, b):
        return jnp.dot(a, b, preferred_element_type=F32)

    marks = flags.astype(BF16)
    count = count_of(within, marks)
    total = jnp.sum(count, 0, keepdims=True)
    start = count_of(before, marks) + count_of(jnp.broadcast_to(total, (16, LANES)).astype(BF16), earlier)
    start = start.astype(jnp.int32)
    place = iota((16, LANES), 0) + 16 * iota((16, LANES), 1)
    table[0:16, :] = start
    table[16:32, :] = HALF - (8 * place - start)
    table[32:48, :] = count.astype(jnp.int32)
    move = fetch([(table, table_s), (table, table_hbm)], sem)
    ranks = count_of(inside, marks)
    row = iota((8, LANES), 0)
    dests, signs = [], []
    for a in range(16):
        sign = flags[8 * a : 8 * a + 8, :].astype(jnp.int32)
        ahead = ranks[8 * a : 8 * a + 8, :].astype(jnp.int32)
        signs.append(sign)
        dests.append(jnp.where(sign > 0, ahead, table[32 + a : 33 + a, :] + row - ahead))
    for a in range(16):
        dest = dests[a]
        dest_t[8 * a : 8 * a + 8, :] = dest
        code = 8 * signs[a]
        for j in range(1, 8):
            code = code + jnp.where(jnp.broadcast_to(dest[j : j + 1, :], (8, LANES)) == row, j, 0)
        code_t[8 * a : 8 * a + 8, :] = code
    wait(move)
    keep = fetch([(dest_t, dest_hbm)], sem)

    def step(c, carry):
        piece(c).wait()
        codes = pltpu.roll(code_t[...], LANES - STEP * c, 1)
        for i in range(STEP):
            r = STEP * c + i
            for a in range(16):
                at = 256 * r + 16 * a
                first = f_ref[pl.ds(at, 8, stride=2), :]
                last = f_ref[pl.ds(at + 1, 8, stride=2), :]
                code = spread(codes[8 * a : 8 * a + 8, :], i)
                sent = jnp.where(code >= 8, last, first)
                sent = jnp.take_along_axis(sent, code & 7, axis=0)
                buf_p[pl.ds(table_s[a, r], 8), :] = sent
                buf_n[pl.ds(table_s[16 + a, r], 8), :] = sent
        return carry

    lax.fori_loop(0, CHUNKS, step, 0)
    wait(fetch([(buf_p, up_hbm), (buf_n.at[PAD - EARLY : PAD], early_hbm), (buf_n.at[0 : PAD - EARLY], late_hbm)], f_sem))
    wait(keep)


def shift_lanes(x, by):
    lane = iota(x.shape, 1)
    if by > 0:
        return jnp.where(lane == 0, 0.0, pltpu.roll(x, 1, 1))
    return jnp.where(lane == LANES - 1, 0.0, pltpu.roll(x, LANES - 1, 1))


def dot(a, b):
    return jnp.dot(a, b, precision=HIGHEST, preferred_element_type=F32)


def sums_kernel(f_hbm, v_hbm, tau_hbm, side_ref, other_ref, wall_hbm, heat_hbm, c_hbm, out_hbm,
                f_ref, v_ref, tau_ref, wall_ref, heat_ref, c_ref, out_ref, sem, f_sem):
    read_v = fetch([(v_hbm, v_ref)], sem)
    piece = pieces(f_hbm, f_ref, f_sem, 2 * LANES)
    for c in range(CHUNKS):
        piece(c).start()
    wait(read_v)
    others = fetch([(tau_hbm, tau_ref), (wall_hbm, wall_ref), (heat_hbm, heat_ref), (c_hbm, c_ref)], sem)
    weight = SPACING**3
    classes = iota((VGRID, LANES), 0).astype(F32)

    def step(c, sums):
        piece(c).wait()
        for i in range(STEP):
            r = STEP * c + i
            sx, sy, sz, sq, n = fields(v_ref[pl.ds(r, 1), :])
            row_4 = (2.0 / 3.0 * sq - 1.0) * weight
            heat = (sq - 2.5) * weight
            moments = jnp.concatenate(
                [jnp.full_like(sx, weight), sx * weight, sy * weight, sz * weight, row_4, sx * heat, sy * heat, sz * heat], 0
            )
            hot = classes == n
            parts = [moments]
            for speed in (sx, sy):
                along = row_4 * jnp.abs(speed)
                parts.append(jnp.where(hot, jnp.where(speed > 0, along, 0.0), 0.0))
                parts.append(jnp.where(hot, jnp.where(speed > 0, 0.0, along), 0.0))
            high, low = split(jnp.concatenate(parts, 0))
            both = jnp.concatenate([f_ref[pl.ds(256 * r + x, LANES, stride=2), :] for x in range(2)], 1)
            f_high, f_low = split(both)
            sums = sums + jnp.dot(
                jnp.concatenate([high, high, low], 1), jnp.concatenate([f_high, f_low, f_high], 0),
                preferred_element_type=F32,
            )
        return sums

    sums = lax.fori_loop(0, CHUNKS, step, jnp.zeros((8 + 4 * VGRID, 2 * LANES), F32))
    wait(others)

    def part(x, k):
        return sums[8 + VGRID * k : 8 + VGRID * (k + 1), LANES * x : LANES * (x + 1)]

    def inverse(tau):
        return 1.0 / (1.0 / tau + classes * SPACING)

    where_vel = 2 * lax.axis_index("chip") + lax.axis_index("core")
    lead = jnp.where(where_vel == 0, 1.0, 0.0)
    core = lax.rem(where_vel, 2)
    before = jnp.where(core == 0, side_ref[1:2, :], other_ref[1:2, :])
    after = jnp.where(core == 0, other_ref[0:1, :], side_ref[0:1, :])
    rows = []
    for x in range(2):
        tau = tau_ref[x : x + 1, :]
        inv = inverse(tau)
        kernels = dot(c_ref[...], inv) * (1.0 / tau)
        moments = sums[0:8, LANES * x : LANES * (x + 1)]
        product = moments * kernels
        gas = jnp.sum(product, 0, keepdims=True)
        wall = product[0:1, :] + lead * heat_ref[x : x + 1, :] * kernels[4:5, :]
        held = jnp.where(wall_ref[x : x + 1, :] == 1, wall, gas) - moments[4:5, :]
        across = part(1, 1) if x == 0 else part(0, 0)
        moved = inv * (across + shift_lanes(part(x, 2), 1) + shift_lanes(part(x, 3), -1))
        out_ref[8 * x : 8 * x + 8, :] = moments
        rows.append(held + jnp.sum(moved, 0, keepdims=True))
    rows.append(jnp.sum(inverse(before) * part(0, 1), 0, keepdims=True))
    rows.append(jnp.sum(inverse(after) * part(1, 0), 0, keepdims=True))
    for j in range(4):
        out_ref[16 + j : 17 + j, :] = rows[j]
    out_ref[20:24, :] = jnp.zeros((4, LANES), F32)
    wait(fetch([(out_ref, out_hbm)], sem))


def merge_kernel(mine_hbm, other_hbm, tau_hbm, payload_hbm, moments_hbm, mine_ref, other_ref, tau_ref, moments_ref, payload, sem):
    wait(fetch([(mine_hbm, mine_ref), (other_hbm, other_ref), (tau_hbm, tau_ref)], sem))
    both = mine_ref[...] + other_ref[...]
    moments_ref[...] = both[0:16, :]
    for k in range(4):
        payload[ROWS * k : ROWS * k + 4, :] = both[16:20, :]
        payload[ROWS * k + 4 : ROWS * k + 6, :] = tau_ref[...]
    block = payload[0 : 4 * ROWS, :]
    for k in range(1, payload.shape[0] // (4 * ROWS)):
        payload[4 * ROWS * k : 4 * ROWS * (k + 1), :] = block
    wait(fetch([(moments_ref, moments_hbm), (payload, payload_hbm)], sem))


def sweep_kernel(f_hbm, v_hbm, mine_hbm, other_hbm, tau_hbm, wall_hbm, heat_hbm, pre_hbm, along_hbm, shape_hbm,
                 f_ref, v_ref, mine_ref, other_ref, tau_ref, wall_ref, heat_ref, pre_ref, along_ref, shape_ref,
                 rhs, cols, sem, f_sem, pre_sem, along_sem):
    first = fetch([(v_hbm, v_ref), (mine_hbm, mine_ref), (other_hbm, other_ref), (tau_hbm, tau_ref), (wall_hbm, wall_ref),
                   (heat_hbm, heat_ref)], sem)
    piece = pieces(f_hbm, f_ref, f_sem, 2 * LANES)
    for c in range(CHUNKS):
        piece(c).start()
    outs = [pieces(pre_ref, pre_hbm, pre_sem, 2 * LANES), pieces(along_ref, along_hbm, along_sem, LANES)]
    rhs[...] = jnp.zeros((LANES, 6 * LANES), F32)
    shape_ref[...] = jnp.zeros((LANES, LANES), F32)
    cols[...] = jnp.zeros((LANES, LANES), F32)
    row = iota((8, LANES), 0)
    classes = iota((VGRID, LANES), 0).astype(F32)
    wait(first)
    for x in range(2):
        part = slice(8 * x, 8 * x + 8)
        moments = mine_ref[part, :] + other_ref[part, :]
        wall = jnp.where(row == 0, moments, jnp.where(row == 4, heat_ref[x : x + 1, :], 0.0))
        relax = 1.0 / tau_ref[x : x + 1, :]
        adjusted = jnp.where(wall_ref[x : x + 1, :] == 1, wall, moments)
        high, low = (p.astype(F32) for p in split(adjusted * relax))
        here = slice(LANES * x, LANES * (x + 1))
        rhs[0:8, here] = high
        rhs[8:16, here] = low
        rhs[16:24, here] = high
        high, low = (p.astype(F32) for p in split(1.0 / (relax + classes * SPACING)))
        here = slice(LANES * (2 + x), LANES * (3 + x))
        rhs[24:48, here] = high
        rhs[48:72, here] = low
    for k in range(2):
        rhs[72:80, LANES * (4 + k) : LANES * (5 + k)] = jnp.where(row == k, 1.0, 0.0)
    rhs_value = rhs[...].astype(BF16)

    def step(c, carry):
        piece(c).wait()
        for i in range(STEP):
            r = STEP * c + i
            sx, sy, sz, sq, n = fields(v_ref[pl.ds(r, 1), :])
            maxwell = jnp.exp(-sq) * math.pi**-1.5
            shape = (sq - 1.5) * maxwell
            heat = SHAKHOV * (sq - 2.5) * maxwell
            high, low = (p.astype(F32) for p in split(jnp.concatenate(
                [maxwell, 2.0 * sx * maxwell, 2.0 * sy * maxwell, 2.0 * sz * maxwell,
                 (1.0 - COOLING) * shape, sx * heat, sy * heat, sz * heat], 0)))
            shape_ref[pl.ds(r, 1), :] = shape
            hot = jnp.where(classes == n, 1.0, 0.0)
            zero = jnp.zeros_like(sx)
            cols[0:80, :] = jnp.concatenate(
                [high, high, low, hot, hot, sx, sy, zero, zero, zero, zero, zero, zero], 0)
            made = jnp.dot(cols[...].T.astype(BF16), rhs_value, preferred_element_type=F32)
            speed_x, speed_y = made[:, 4 * LANES : 5 * LANES], made[:, 5 * LANES : 6 * LANES]
            rows = [f_ref[pl.ds(256 * r + x, LANES, stride=2), :] for x in range(2)]
            along_x, along_y = jnp.abs(speed_x), jnp.abs(speed_y)
            ahead = speed_x > 0
            for x in range(2):
                upwind_y = jnp.where(speed_y > 0, shift_lanes(rows[x], 1), shift_lanes(rows[x], -1))
                near = jnp.where(ahead, 0.0, rows[1]) if x == 0 else jnp.where(ahead, rows[0], 0.0)
                inv = made[:, LANES * (2 + x) : LANES * (3 + x)]
                value = (made[:, LANES * x : LANES * (x + 1)] + along_x * near + along_y * upwind_y) * inv
                pre_ref[pl.ds(256 * r + x, LANES, stride=2), :] = value
            at = pl.ds(pl.multiple_of(LANES * r, LANES), LANES)
            along_ref[at, :] = speed_x * jnp.where(ahead, made[:, 2 * LANES : 3 * LANES], made[:, 3 * LANES : 4 * LANES])
        for out in outs:
            out(c).start()
        return carry

    lax.fori_loop(0, CHUNKS, step, 0)
    shape_ref[...] = shape_ref[...].T
    keep = fetch([(shape_ref, shape_hbm)], sem)
    wait(keep)
    for c in range(CHUNKS):
        for out in outs:
            out(c).wait()


def finish_kernel(pre_hbm, along_hbm, shape_hbm, dest_hbm, table_hbm, y_hbm, up_hbm, early_hbm, late_hbm, out_hbm, corr_ref,
                  pre_ref, along_ref, shape_t, dest_t, table_s, y_ref, buf_p, buf_n, kept, out_ref, sem, pre_sem, along_sem, out_sem):
    copies = fetch([(y_hbm, y_ref), (table_hbm, table_s), (shape_hbm, shape_t), (dest_hbm, dest_t), (up_hbm, buf_p),
                    (early_hbm, buf_n.at[PAD - EARLY : PAD]), (late_hbm, buf_n.at[0 : PAD - EARLY])], sem)
    ins = [pieces(pre_hbm, pre_ref, pre_sem, 2 * LANES), pieces(along_hbm, along_ref, along_sem, LANES)]
    done = pieces(out_ref, out_hbm, out_sem, 2 * LANES)
    for c in range(CHUNKS):
        for piece in ins:
            piece(c).start()
    copies[0].wait()

    def take(device, j):
        return y_ref[pl.ds(ROWS * device + j, 64, stride=ROWS), :]

    place = iota((64, LANES), 0)

    def lower(x):
        return jnp.where(place == 0, 0.0, pltpu.roll(x, 1, 0))

    def upper(x):
        return jnp.where(place == 63, 0.0, pltpu.roll(x, 63, 0))

    def over_vel(j):
        return take(0, j) + take(64, j)

    even = over_vel(0) + lower(over_vel(3))
    odd = over_vel(1) + upper(over_vel(2))
    middle_even = COOLING / take(0, 4) + 4.0
    middle_odd = COOLING / take(0, 5) + 4.0

    def operate(e, o):
        image_e = middle_even * e - (lower(o) + o + shift_lanes(e, 1) + shift_lanes(e, -1))
        image_o = middle_odd * o - (e + upper(e) + shift_lanes(o, 1) + shift_lanes(o, -1))
        return image_e, image_o

    def inner(a, b):
        total = jnp.sum(a[0] * b[0] + a[1] * b[1], 0, keepdims=True)
        return jnp.sum(total, 1, keepdims=True)

    residual = (even, odd)
    direction = residual
    found = (jnp.zeros_like(even), jnp.zeros_like(odd))
    norm_now = inner(residual, residual)
    for rounds in range(ITERS):
        image = operate(*direction)
        step_size = norm_now / inner(direction, image)
        found = tuple(v + step_size * d for v, d in zip(found, direction))
        if rounds + 1 < ITERS:
            residual = tuple(r - step_size * i for r, i in zip(residual, image))
            norm_next = inner(residual, residual)
            direction = tuple(r + norm_next / norm_now * d for r, d in zip(residual, direction))
            norm_now = norm_next
    kept[0:64, :] = found[0]
    kept[64:128, :] = found[1]
    where_space = lax.axis_index("space")
    corr_ref[0:1, :] = kept[pl.ds(where_space, 1), :]
    corr_ref[1:2, :] = kept[pl.ds(64 + where_space, 1), :]
    wait(copies[1:])
    corr = [jnp.broadcast_to(corr_ref[x : x + 1, :], (8, LANES)) for x in range(2)]
    row = iota((8, LANES), 0)

    def step(c, carry):
        for piece in ins:
            piece(c).wait()
        shapes = pltpu.roll(shape_t[...], LANES - STEP * c, 1)
        dests = pltpu.roll(dest_t[...], LANES - STEP * c, 1)
        for i in range(STEP):
            r = STEP * c + i
            for a in range(16):
                at = 128 * r + 8 * a
                here = pl.ds(pl.multiple_of(at, 8), 8)
                halo = jnp.where(row < table_s[32 + a, r], buf_p[pl.ds(table_s[a, r], 8), :],
                                 buf_n[pl.ds(table_s[16 + a, r], 8), :])
                along = along_ref[here, :]
                moved = along * jnp.take_along_axis(halo, spread(dests[8 * a : 8 * a + 8, :], i), axis=0)
                ahead = along > 0
                shape = spread(shapes[8 * a : 8 * a + 8, :], i)
                near = pl.ds(2 * at, 8, stride=2)
                far = pl.ds(2 * at + 1, 8, stride=2)
                out_ref[near, :] = pre_ref[near, :] + jnp.where(ahead, moved, 0.0) + shape * corr[0]
                out_ref[far, :] = pre_ref[far, :] - jnp.where(ahead, 0.0, moved) + shape * corr[1]
        done(c).start()
        return carry

    lax.fori_loop(0, CHUNKS, step, 0)
    for c in range(CHUNKS):
        done(c).wait()


def vmem(shape, dtype=F32):
    return pltpu.VMEM(shape, dtype)


def struct(shape, dtype=F32):
    return jax.ShapeDtypeStruct(shape, dtype)


IN_HBM = pl.BlockSpec(memory_space=pltpu.HBM)
IN_VMEM = pl.BlockSpec(memory_space=pltpu.VMEM)
DMA = pltpu.SemaphoreType.DMA
INT = jnp.int32


def call(kernel, outs, scratch, args, flops, out_specs=None, local=(), mib=None, alias=None):
    return pl.pallas_call(
        kernel,
        out_shape=outs,
        in_specs=[IN_VMEM if i in local else IN_HBM for i in range(len(args))],
        out_specs=jax.tree.map(lambda _: IN_HBM, outs) if out_specs is None else out_specs,
        scratch_shapes=scratch,
        input_output_aliases=alias or {},
        compiler_params=pltpu.CompilerParams(vmem_limit_bytes=None if mib is None else mib << 20),
        cost_estimate=pl.CostEstimate(flops=flops, bytes_accessed=8 << 20, transcendentals=0),
    )(*args)


def program(distribution, vel_index, collision_time, wall_flags, wall_temp):
    space = lax.axis_size("space")
    chips = lax.axis_size("chip")
    up = [(i, i + 1) for i in range(space - 1)]
    down = [(j, i) for i, j in up]
    both = []
    for v in range(2 * chips):
        both += [(v * space + i, v * space + j) for i, j in (up if v % 2 == 0 else down)]

    swap = [(0, 1), (1, 0)]
    ring = []
    for c in range(chips):
        for k in range(space):
            ring.append((c * space + k, c * space + k + 1 if k % 2 == 0 else (c + 1) % chips * space + k - 1))
    flat = distribution.reshape(2 * SLOTS, LANES)
    ids = vel_index.reshape(BLOCKS, LANES)
    small, square, whole, halves = (2, LANES), (LANES, LANES), (2 * SLOTS, LANES), (SLOTS, LANES)
    side = lax.ppermute(collision_time, ("chip", "core", "space"), both)
    rows_up, rows_early, rows_late, dest, table = call(
        compact_kernel,
        (struct((PAD, LANES)), struct((EARLY, LANES)), struct((PAD - EARLY, LANES)), struct(square, INT), struct((48, LANES), INT)),
        [vmem(whole), vmem((BLOCKS, LANES), INT), vmem(square), vmem(square, INT), vmem(square, INT), vmem((48, LANES), INT),
         vmem((PAD, LANES)), vmem((PAD, LANES)), pltpu.SMEM((48, LANES), INT), DMA((2,)), DMA((CHUNKS,))],
        (flat, ids), 1 << 20,
    )
    halo_up = lax.ppermute(rows_up, "space", up)
    halo_early = lax.ppermute(rows_early, "space", down)
    side_other = lax.ppermute(side, "core", swap)
    sums = call(
        sums_kernel, struct((24, LANES)),
        [vmem(whole), vmem((BLOCKS, LANES), INT), vmem(small), vmem(small, INT), vmem(small),
         vmem((8, VGRID)), vmem((24, LANES)), DMA((4,)), DMA((CHUNKS,))],
        (flat, ids, collision_time, side, side_other, wall_flags, wall_temp, jnp.asarray(class_constants())), 1 << 30,
        local=(3, 4),
    )
    sums_other = lax.ppermute(sums, "core", swap)
    gather = ROWS * chips * space
    payload, moments = call(
        merge_kernel, (struct((gather, LANES)), struct((16, LANES))),
        [vmem((24, LANES)), vmem((24, LANES)), vmem(small), vmem((16, LANES)), vmem((gather, LANES)), DMA((3,))],
        (sums, sums_other, collision_time), 1 << 16,
    )
    gathered = lax.all_to_all(payload.reshape(chips * space, 1, ROWS * LANES), ("chip", "space"), 0, 0, tiled=True)
    moments_other = lax.ppermute(lax.ppermute(moments, ("chip", "space"), ring), ("chip", "space"), ring)
    halo_late = lax.ppermute(rows_late, "space", down)
    pre, along, shape = call(
        sweep_kernel,
        (struct(whole), struct(halves), struct(square)),
        [vmem(whole), vmem((BLOCKS, LANES), INT), vmem((16, LANES)), vmem((16, LANES)), vmem(small), vmem(small, INT), vmem(small),
         vmem(whole), vmem(halves), vmem(square), vmem((LANES, 6 * LANES)), vmem(square),
         DMA((6,)), DMA((CHUNKS,)), DMA((CHUNKS,)), DMA((CHUNKS,))],
        (flat, ids, moments, moments_other, collision_time, wall_flags, wall_temp), 1 << 30,
    )
    result, correction = call(
        finish_kernel, (struct(whole), struct(small)),
        [vmem(whole), vmem(halves), vmem(square), vmem(square, INT), pltpu.SMEM((48, LANES), INT), vmem((gather, LANES)),
         vmem((PAD, LANES)), vmem((PAD, LANES)), vmem(square), vmem(whole), DMA((7,))] + [DMA((CHUNKS,))] * 3,
        (pre, along, shape, dest, table, gathered.reshape(gather, LANES), halo_up, halo_early, halo_late), 1 << 24,
        (IN_HBM, IN_VMEM),
    )
    return result.reshape(SLOTS, 2, LANES), correction


def solution(mesh):
    vel, space = mesh.devices.shape
    mesh = jax.sharding.Mesh(mesh.devices.reshape(vel // 2, 2, space), ("chip", "core", "space"))
    cores = ("chip", "core")
    placed = (P(cores, "space", None), P(cores), P("space", None), P("space", None), P("space", None))
    return jax.shard_map(
        program,
        mesh=mesh,
        in_specs=placed,
        out_specs=(P(cores, "space", None), P("space", None)),
        check_vma=False,
    )
```

time: 110 us -> 93.6 us (0.85)
  the two profiles are of different devices: /device:TPU:1 before, /device:TPU:4 now
where the time goes in v2:
time: 93.6 us; the launch traced here: 93.2 us
  starting transfers between devices  49.8 us (53%)
  Pallas kernels  28.3 us (30%)
  waiting for transfers between devices  11.2 us (12%)
  local copies, waits for them, and re-layouts  3.1 us (3%)
    pallas_call x5, Pallas kernels, call(): pl.pallas_call(kernel, out_shape=outs, in_specs=[IN_VMEM if i in local el...  28.3 us
    all_to_all x1, starting transfers between devices, program(): lax.all_to_all(payload.reshape(chips * space, 1, ROWS * LANES), ('chip',...  18.3 us
    ppermute x1, starting transfers between devices, program(): lax.ppermute(lax.ppermute(moments, ('chip', 'space'), ring), ('chip', 'sp...  17.6 us
    ppermute x1, waiting for transfers between devices, program(): lax.ppermute(moments, ('chip', 'space'), ring)  3.63 us
    ppermute x1, starting transfers between devices, program(): side = lax.ppermute(collision_time, ('chip', 'core', 'space'), both)  3.49 us
    ppermute x1, starting transfers between devices, program(): halo_early = lax.ppermute(rows_early, 'space', down)  3.37 us
    ppermute x1, waiting for transfers between devices, program(): lax.ppermute(lax.ppermute(moments, ('chip', 'space'), ring), ('chip', 'sp...  3.31 us
    unnamed x20, local copies, waits for them, and re-layouts  3.1 us
  transfers between devices with their start and end apart: 9, of which 4 were waited for; matrix products, arithmetic and copies ran while one was open for 0% of the time, Pallas kernels for 23%

profile of v2, /device:TPU:4, one launch (start us, length us, event | category | flops | bytes accessed | tf_op | source)
XLA Modules:
  0.0 93.2 jit_solution(4895030323959411427)
XLA Ops:
  0.6 3.5 %collective-permute-start = (f32[2,128]{1,0:T(2,128)}, f32[2,128]{1,0:T(2,128)S(1)}, u32[]{:S(2)}, u32[]{:S(2)}) collective-permute-start(f32[2,128]{1,0:T(2,128)} %tau_hbm.5), channel_id=1, source_target_pairs={{0,1},{1,2},{2,3},{3,4},{4,5},{5,6},{6,7},{7,8},{8,9},{9,10},{10,1... | collective-permute-start | bytes 3080 | tf_op jit(solution)/shard_map/ppermute | solution.py:477
  4.1 3.1 %collective-permute-done.side_ref = f32[2,128]{1,0:T(2,128)S(1)} collective-permute-done((f32[2,128]{1,0:T(2,128)}, f32[2,128]{1,0:T(2,128)S(1)}, u32[]{:S(2)}, u32[]{:S(2)}) %collective-permute-start) | collective-permute-done | bytes 1056 | tf_op jit(solution)/shard_map/ppermute | solution.py:477
  7.2 0.0 copy-start.8
  7.2 0.0 collective-permute-start.1
  7.2 6.5 %shard_map.80 = (f32[1736,128]{1,0:T(8,128)}, f32[1000,128]{1,0:T(8,128)}, f32[736,128]{1,0:T(8,128)}, s32[128,128]{1,0:T(8,128)}, s32[48,128]{1,0:T(8,128)}) custom-call(f32[6912,128]{1,0:T(8,128)} %bitcast.5, s32[27,128]{1,0:T(8,128)} %bitcast.10), custom_call_target="tpu_custom_call" | custom-call | flops 1048576 | bytes 8388608 | tf_op jit(solution)/shard_map/pallas_call | solution.py:448
  13.7 0.0 copy-start.5
  13.7 0.0 copy-start.6
  13.7 2.7 %collective-permute-start.5 = (f32[1736,128]{1,0:T(8,128)}, f32[1736,128]{1,0:T(8,128)S(1)}, u32[]{:S(2)}, u32[]{:S(2)}) collective-permute-start(f32[1736,128]{1,0:T(8,128)} %get-tuple-element.21), channel_id=1, source_target_pairs={{0,1},{1,2},{2,3},{3,4},{4,5},{5,6},{6,7},{7,8},{8,9},{9,10},{10,1... | collective-permute-start | bytes 2666504 | tf_op jit(solution)/shard_map/ppermute | solution.py:485
  16.5 0.0 collective-permute-done.1.other_ref
  16.5 0.0 copy-done.8
  16.5 0.0 copy-start.9
  16.5 0.6 copy-done.9
  17.0 5.8 %shard_map.77.mine_hbm = f32[24,128]{1,0:T(8,128)} custom-call(f32[6912,128]{1,0:T(8,128)} %bitcast.6, s32[27,128]{1,0:T(8,128)} %bitcast.11, f32[2,128]{1,0:T(2,128)} %tau_hbm.5, f32[2,128]{1,0:T(2,128)} %copy-done.8, f32[2,128]{1,0:T(2,128)} %copy-done.9, s32[2,128]{1,0:T(2,128)} %wall_hbm.3, f32[2,128]{1,0:T(2,128)} %heat_hbm.3, f32[8,24]{1,0:T(8,128)} %constant.2.clone.c_hbm), custom_call_target="tpu_custom_call" | custom-call | flops 1073741824 | bytes 8388608 | tf_op jit(solution)/shard_map/pallas_call | solution.py:448
  22.9 0.3 collective-permute-start.2
  23.2 1.2 %collective-permute-done.2.other_hbm = f32[24,128]{1,0:T(8,128)S(1)} collective-permute-done((f32[24,128]{1,0:T(8,128)}, f32[24,128]{1,0:T(8,128)S(1)}, u32[]{:S(2)}, u32[]{:S(2)}) %collective-permute-start.2) | collective-permute-done | bytes 12320 | tf_op jit(solution)/shard_map/ppermute | solution.py:495
  24.3 0.0 copy-start.4
  24.3 0.6 copy-done.4
  24.9 1.5 %shard_map.78 = (f32[768,128]{1,0:T(8,128)}, f32[16,128]{1,0:T(8,128)}) custom-call(f32[24,128]{1,0:T(8,128)} %shard_map.77.mine_hbm, f32[24,128]{1,0:T(8,128)} %copy-done.4, f32[2,128]{1,0:T(2,128)} %tau_hbm.5), custom_call_target="tpu_custom_call" | custom-call | flops 65536 | bytes 8388608 | tf_op jit(solution)/shard_map/pallas_call | solution.py:448
  26.5 18.3 %all-to-all-start = ((f32[128,1,768]{2,1,0:T(1,128)}), f32[128,1,768]{2,1,0:T(1,128)S(1)}, u32[]{:S(2)}, u32[]{:S(2)}) async-start(f32[128,1,768]{2,1,0:T(1,128)} %bitcast.9), calls=%async_computation | async-start | bytes 786432 | tf_op jit(solution)/shard_map/all_to_all | solution.py:502
  44.8 0.0 copy-done.5
  44.8 3.4 %collective-permute-start.6 = (f32[1000,128]{1,0:T(8,128)S(1)}, f32[1000,128]{1,0:T(8,128)S(1)}, u32[]{:S(2)}, u32[]{:S(2)}) collective-permute-start(f32[1000,128]{1,0:T(8,128)S(1)} %copy-done.5), channel_id=1, source_target_pairs={{1,0},{2,1},{3,2},{4,3},{5,4},{6,5},{7,6},{8,7},{9,8},{10,9},{11,1... | collective-permute-start | bytes 1536008 | tf_op jit(solution)/shard_map/ppermute | solution.py:486
  48.1 0.0 copy-done.6
  48.2 2.5 %collective-permute-start.7 = (f32[736,128]{1,0:T(8,128)S(1)}, f32[736,128]{1,0:T(8,128)S(1)}, u32[]{:S(2)}, u32[]{:S(2)}) collective-permute-start(f32[736,128]{1,0:T(8,128)S(1)} %copy-done.6), channel_id=1, source_target_pairs={{1,0},{2,1},{3,2},{4,3},{5,4},{6,5},{7,6},{8,7},{9,8},{10,9},{11,1... | collective-permute-start | bytes 1130504 | tf_op jit(solution)/shard_map/ppermute | solution.py:504
  50.6 1.5 %collective-permute-start.3 = (f32[16,128]{1,0:T(8,128)}, f32[16,128]{1,0:T(8,128)S(1)}, u32[]{:S(2)}, u32[]{:S(2)}) collective-permute-start(f32[16,128]{1,0:T(8,128)} %get-tuple-element.14.mine_hbm), channel_id=1, source_target_pairs={{0,1},{1,128},{2,3},{3,130},{4,5},{5,132},{6,7},{7,134},{8,9},{9,1... | collective-permute-start | bytes 24584 | tf_op jit(solution)/shard_map/ppermute | solution.py:503
  52.2 3.6 %collective-permute-done.3 = f32[16,128]{1,0:T(8,128)S(1)} collective-permute-done((f32[16,128]{1,0:T(8,128)}, f32[16,128]{1,0:T(8,128)S(1)}, u32[]{:S(2)}, u32[]{:S(2)}) %collective-permute-start.3) | collective-permute-done | bytes 8224 | tf_op jit(solution)/shard_map/ppermute | solution.py:503
  55.8 17.6 %collective-permute-start.4 = (f32[16,128]{1,0:T(8,128)S(1)}, f32[16,128]{1,0:T(8,128)S(1)}, u32[]{:S(2)}, u32[]{:S(2)}) collective-permute-start(f32[16,128]{1,0:T(8,128)S(1)} %collective-permute-done.3), channel_id=1, source_target_pairs={{0,1},{1,128},{2,3},{3,130},{4,5},{5,132},{6,7},{7,134},{8,9},{9,1... | collective-permute-start | bytes 24584 | tf_op jit(solution)/shard_map/ppermute | solution.py:503
  73.4 3.3 %collective-permute-done.4.other_hbm = f32[16,128]{1,0:T(8,128)S(1)} collective-permute-done((f32[16,128]{1,0:T(8,128)S(1)}, f32[16,128]{1,0:T(8,128)S(1)}, u32[]{:S(2)}, u32[]{:S(2)}) %collective-permute-start.4) | collective-permute-done | bytes 8224 | tf_op jit(solution)/shard_map/ppermute | solution.py:503
  76.7 0.0 copy-start.7
  76.7 0.6 copy-done.7
  77.3 7.1 %shard_map.79 = (f32[6912,128]{1,0:T(8,128)}, f32[3456,128]{1,0:T(8,128)}, f32[128,128]{1,0:T(8,128)}) custom-call(f32[6912,128]{1,0:T(8,128)} %bitcast.7, s32[27,128]{1,0:T(8,128)} %bitcast.12, f32[16,128]{1,0:T(8,128)} %get-tuple-element.14.mine_hbm, f32[16,128]{1,0:T(8,128)} %copy-done.7, f32[2,128]{1,0:T(2,128)} %tau_hbm.5, s32[2,128]{1,0:T(2,128)} %wall_hbm.3, ...), custom_call_target="tpu_custom_call" | custom-call | flops 1073741824 | bytes 8388608 | tf_op jit(solution)/shard_map/pallas_call | solution.py:448
  84.5 0.0 collective-permute-done.7.late_hbm
  84.5 0.0 copy-start.3
  84.5 0.0 collective-permute-done.6.early_hbm
  84.5 0.0 copy-start.2
  84.5 0.0 all-to-all-done
  84.5 0.0 copy-start
  84.5 0.0 collective-permute-done.5.up_hbm
  84.5 0.0 copy-start.1
  84.5 0.7 copy-done.3
  85.2 0.2 copy-done.2
  85.4 0.1 copy-done
  85.5 0.3 copy-done.1
  85.9 7.3 %shard_map.81 = (f32[6912,128]{1,0:T(8,128)}, f32[2,128]{1,0:T(2,128)}) custom-call(f32[6912,128]{1,0:T(8,128)} %get-tuple-element.15.pre_hbm, f32[3456,128]{1,0:T(8,128)} %get-tuple-element.16.along_hbm, f32[128,128]{1,0:T(8,128)} %get-tuple-element.17.shape_hbm, s32[128,128]{1,0:T(8,128)} %get-tuple-element.18.dest_hbm, ...), custom_call_target="tpu_custom_call" | custom-call | flops 16777216 | bytes 8388608 | tf_op jit(solution)/shard_map/pallas_call | solution.py:448
Async XLA Ops:
  0.6 6.6 %collective-permute-start = (f32[2,128]{1,0:T(2,128)}, f32[2,128]{1,0:T(2,128)S(1)}, u32[]{:S(2)}, u32[]{:S(2)}) collective-permute-start(f32[2,128]{1,0:T(2,128)} %tau_hbm.5), channel_id=1, source_target_pairs={{0,1},{1,2},{2,3},{3,4},{4,5},{5,6},{6,7},{7,8},{8,9},{9,10},{10,1... | collective-permute-start | bytes 3080 | tf_op jit(solution)/shard_map/ppermute | solution.py:477
  7.2 9.3 %copy-start.8 = (f32[2,128]{1,0:T(2,128)}, f32[2,128]{1,0:T(2,128)S(1)}, u32[]{:S(2)}) copy-start(f32[2,128]{1,0:T(2,128)S(1)} %collective-permute-done.side_ref) | copy-start | bytes 3076
  7.2 9.2 %collective-permute-start.1 = (f32[2,128]{1,0:T(2,128)S(1)}, f32[2,128]{1,0:T(2,128)S(1)}, u32[]{:S(2)}, u32[]{:S(2)}) collective-permute-start(f32[2,128]{1,0:T(2,128)S(1)} %collective-permute-done.side_ref), channel_id=1, source_target_pairs={{0,64},{64,0},{1,65},{65,1},{2,66},{66,2},{3,67},{67,3},{4,68},{68... | collective-permute-start | bytes 3080 | tf_op jit(solution)/shard_map/ppermute | solution.py:487
  13.7 31.1 %copy-start.5 = (f32[1000,128]{1,0:T(8,128)S(1)}, f32[1000,128]{1,0:T(8,128)}, u32[]{:S(2)}) copy-start(f32[1000,128]{1,0:T(8,128)} %get-tuple-element.22) | copy-start | bytes 1536004
  13.7 34.4 %copy-start.6 = (f32[736,128]{1,0:T(8,128)S(1)}, f32[736,128]{1,0:T(8,128)}, u32[]{:S(2)}) copy-start(f32[736,128]{1,0:T(8,128)} %get-tuple-element.23) | copy-start | bytes 1130500
  13.7 70.8 %collective-permute-start.5 = (f32[1736,128]{1,0:T(8,128)}, f32[1736,128]{1,0:T(8,128)S(1)}, u32[]{:S(2)}, u32[]{:S(2)}) collective-permute-start(f32[1736,128]{1,0:T(8,128)} %get-tuple-element.21), channel_id=1, source_target_pairs={{0,1},{1,2},{2,3},{3,4},{4,5},{5,6},{6,7},{7,8},{8,9},{9,10},{10,1... | collective-permute-start | bytes 2666504 | tf_op jit(solution)/shard_map/ppermute | solution.py:485
  16.5 0.6 copy-start.9
  22.9 1.5 %collective-permute-start.2 = (f32[24,128]{1,0:T(8,128)}, f32[24,128]{1,0:T(8,128)S(1)}, u32[]{:S(2)}, u32[]{:S(2)}) collective-permute-start(f32[24,128]{1,0:T(8,128)} %shard_map.77.mine_hbm), channel_id=1, source_target_pairs={{0,64},{64,0},{1,65},{65,1},{2,66},{66,2},{3,67},{67,3},{4,68},{68... | collective-permute-start | bytes 36872 | tf_op jit(solution)/shard_map/ppermute | solution.py:495
  24.3 0.6 copy-start.4
  26.5 58.0 %all-to-all-start = ((f32[128,1,768]{2,1,0:T(1,128)}), f32[128,1,768]{2,1,0:T(1,128)S(1)}, u32[]{:S(2)}, u32[]{:S(2)}) async-start(f32[128,1,768]{2,1,0:T(1,128)} %bitcast.9), calls=%async_computation | async-start | bytes 786432 | tf_op jit(solution)/shard_map/all_to_all | solution.py:502
  44.8 39.7 %collective-permute-start.6 = (f32[1000,128]{1,0:T(8,128)S(1)}, f32[1000,128]{1,0:T(8,128)S(1)}, u32[]{:S(2)}, u32[]{:S(2)}) collective-permute-start(f32[1000,128]{1,0:T(8,128)S(1)} %copy-done.5), channel_id=1, source_target_pairs={{1,0},{2,1},{3,2},{4,3},{5,4},{6,5},{7,6},{8,7},{9,8},{10,9},{11,1... | collective-permute-start | bytes 1536008 | tf_op jit(solution)/shard_map/ppermute | solution.py:486
  48.2 36.3 %collective-permute-start.7 = (f32[736,128]{1,0:T(8,128)S(1)}, f32[736,128]{1,0:T(8,128)S(1)}, u32[]{:S(2)}, u32[]{:S(2)}) collective-permute-start(f32[736,128]{1,0:T(8,128)S(1)} %copy-done.6), channel_id=1, source_target_pairs={{1,0},{2,1},{3,2},{4,3},{5,4},{6,5},{7,6},{8,7},{9,8},{10,9},{11,1... | collective-permute-start | bytes 1130504 | tf_op jit(solution)/shard_map/ppermute | solution.py:504
  50.6 5.2 %collective-permute-start.3 = (f32[16,128]{1,0:T(8,128)}, f32[16,128]{1,0:T(8,128)S(1)}, u32[]{:S(2)}, u32[]{:S(2)}) collective-permute-start(f32[16,128]{1,0:T(8,128)} %get-tuple-element.14.mine_hbm), channel_id=1, source_target_pairs={{0,1},{1,128},{2,3},{3,130},{4,5},{5,132},{6,7},{7,134},{8,9},{9,1... | collective-permute-start | bytes 24584 | tf_op jit(solution)/shard_map/ppermute | solution.py:503
  55.8 20.9 %collective-permute-start.4 = (f32[16,128]{1,0:T(8,128)S(1)}, f32[16,128]{1,0:T(8,128)S(1)}, u32[]{:S(2)}, u32[]{:S(2)}) collective-permute-start(f32[16,128]{1,0:T(8,128)S(1)} %collective-permute-done.3), channel_id=1, source_target_pairs={{0,1},{1,128},{2,3},{3,130},{4,5},{5,132},{6,7},{7,134},{8,9},{9,1... | collective-permute-start | bytes 24584 | tf_op jit(solution)/shard_map/ppermute | solution.py:503
  76.7 0.6 copy-start.7
  84.5 0.7 copy-start.3
  84.5 0.9 copy-start.2
  84.5 1.0 %copy-start = (f32[128,1,768]{2,1,0:T(1,128)}, f32[128,1,768]{2,1,0:T(1,128)S(1)}, u32[]{:S(2)}) copy-start(f32[128,1,768]{2,1,0:T(1,128)S(1)} %all-to-all-done) | copy-start | bytes 1179652
  84.5 1.3 %copy-start.1 = (f32[1736,128]{1,0:T(8,128)}, f32[1736,128]{1,0:T(8,128)S(1)}, u32[]{:S(2)}) copy-start(f32[1736,128]{1,0:T(8,128)S(1)} %collective-permute-done.5.up_hbm) | copy-start | bytes 2666500

commit v3 on v2

--- a/solution.py
+++ b/solution.py
@@ -23,7 +23,8 @@
 BLOCKS = SLOTS // LANES
 PAD = HALF + 8
 ROWS = 6
-EARLY = 1000
+EARLY = 760
+THIRD = 520
 CHUNKS = 9
 STEP = BLOCKS // CHUNKS
 BF16 = jnp.bfloat16
@@ -101,7 +102,7 @@
 
 
 def compact_kernel(f_hbm, v_hbm, up_hbm, early_hbm, late_hbm, dest_hbm, table_hbm,
-                   f_ref, v_ref, square, code_t, dest_t, table, buf_p, buf_n, table_s, sem, f_sem):
+                   f_ref, v_ref, square, code_t, dest_t, table, buf_p, buf_n, table_s, sem, f_sem, out_sem):
     read_v = fetch([(v_hbm, v_ref)], sem)
     piece = pieces(f_hbm, f_ref, f_sem, 2 * LANES)
     for c in range(CHUNKS):
@@ -148,6 +149,11 @@
     wait(move)
     keep = fetch([(dest_t, dest_hbm)], sem)
 
+    bounds = [0, THIRD, 2 * THIRD, 3 * THIRD, PAD]
+    out_up = [pltpu.make_async_copy(buf_p.at[a:b], up_hbm.at[a:b], out_sem.at[k]) for k, (a, b) in enumerate(zip(bounds, bounds[1:]))]
+    out_early = pltpu.make_async_copy(buf_n.at[PAD - EARLY : PAD], early_hbm, out_sem.at[4])
+    out_late = pltpu.make_async_copy(buf_n.at[0 : PAD - EARLY], late_hbm, out_sem.at[5])
+
     def step(c, carry):
         piece(c).wait()
         codes = pltpu.roll(code_t[...], LANES - STEP * c, 1)
@@ -162,10 +168,24 @@
                 sent = jnp.take_along_axis(sent, code & 7, axis=0)
                 buf_p[pl.ds(table_s[a, r], 8), :] = sent
                 buf_n[pl.ds(table_s[16 + a, r], 8), :] = sent
+        now, then = table_s[0, STEP * c + STEP], table_s[0, STEP * c]
+        for k in range(3):
+            @pl.when((now >= THIRD * (k + 1)) & (then < THIRD * (k + 1)))
+            def _():
+                out_up[k].start()
+
+        now, then = table_s[16, STEP * c + STEP], table_s[16, STEP * c]
+
+        @pl.when((now <= HALF - EARLY) & (then > HALF - EARLY))
+        def _():
+            out_early.start()
+
         return carry
 
     lax.fori_loop(0, CHUNKS, step, 0)
-    wait(fetch([(buf_p, up_hbm), (buf_n.at[PAD - EARLY : PAD], early_hbm), (buf_n.at[0 : PAD - EARLY], late_hbm)], f_sem))
+    out_up[3].start()
+    out_late.start()
+    wait([*out_up, out_early, out_late])
     wait(keep)
 
 
@@ -444,7 +464,7 @@
 INT = jnp.int32
 
 
-def call(kernel, outs, scratch, args, flops, out_specs=None, local=(), mib=None, alias=None):
+def call(kernel, outs, scratch, args, flops, out_specs=None, local=(), alias=None):
     return pl.pallas_call(
         kernel,
         out_shape=outs,
@@ -452,7 +472,7 @@
         out_specs=jax.tree.map(lambda _: IN_HBM, outs) if out_specs is None else out_specs,
         scratch_shapes=scratch,
         input_output_aliases=alias or {},
-        compiler_params=pltpu.CompilerParams(vmem_limit_bytes=None if mib is None else mib << 20),
+        compiler_params=pltpu.CompilerParams(vmem_limit_bytes=52 << 20),
         cost_estimate=pl.CostEstimate(flops=flops, bytes_accessed=8 << 20, transcendentals=0),
     )(*args)
 
@@ -479,7 +499,7 @@
         compact_kernel,
         (struct((PAD, LANES)), struct((EARLY, LANES)), struct((PAD - EARLY, LANES)), struct(square, INT), struct((48, LANES), INT)),
         [vmem(whole), vmem((BLOCKS, LANES), INT), vmem(square), vmem(square, INT), vmem(square, INT), vmem((48, LANES), INT),
-         vmem((PAD, LANES)), vmem((PAD, LANES)), pltpu.SMEM((48, LANES), INT), DMA((2,)), DMA((CHUNKS,))],
+         vmem((PAD, LANES)), vmem((PAD, LANES)), pltpu.SMEM((48, LANES), INT), DMA((2,)), DMA((CHUNKS,)), DMA((6,))],
         (flat, ids), 1 << 20,
     )
     halo_up = lax.ppermute(rows_up, "space", up)

time: 93.6 us -> 88.1 us (0.941)
  Pallas kernels: 28.3 us -> 24.2 us
  local copies, waits for them, and re-layouts: 3.1 us -> 2 us
    pallas_call x5, Pallas kernels: 28.3 us -> 24.2 us  [call(): pl.pallas_call(kernel, out_shape=outs, in_specs=[IN_VMEM if i in local el...]
    unnamed x20 -> x14, local copies, waits for them, and re-layouts: 3.1 us -> 2 us
  transfers between devices with their start and end apart: 9 -> 9, of which waited for: 4 -> 4; matrix products, arithmetic and copies ran while one was open for 0% -> 0% of each run, Pallas kernels for 23% -> 20%
where the time goes in v3:
time: 88.1 us; the launch traced here: 87.7 us
  starting transfers between devices  49.9 us (57%)
  Pallas kernels  24.2 us (27%)
  waiting for transfers between devices  10.8 us (12%)
  local copies, waits for them, and re-layouts  2 us (2%)
    pallas_call x5, Pallas kernels, call(): pl.pallas_call(kernel, out_shape=outs, in_specs=[IN_VMEM if i in local el...  24.2 us
    all_to_all x1, starting transfers between devices, program(): lax.all_to_all(payload.reshape(chips * space, 1, ROWS * LANES), ('chip',...  18.3 us
    ppermute x1, starting transfers between devices, program(): lax.ppermute(lax.ppermute(moments, ('chip', 'space'), ring), ('chip', 'sp...  17.8 us
    ppermute x1, starting transfers between devices, program(): side = lax.ppermute(collision_time, ('chip', 'core', 'space'), both)  3.62 us
    ppermute x1, waiting for transfers between devices, program(): lax.ppermute(moments, ('chip', 'space'), ring)  3.48 us
    ppermute x1, starting transfers between devices, program(): halo_late = lax.ppermute(rows_late, 'space', down)  3.37 us
    ppermute x1, waiting for transfers between devices, program(): lax.ppermute(lax.ppermute(moments, ('chip', 'space'), ring), ('chip', 'sp...  3.3 us
    ppermute x1, waiting for transfers between devices, program(): side = lax.ppermute(collision_time, ('chip', 'core', 'space'), both)  3.08 us
  transfers between devices with their start and end apart: 9, of which 4 were waited for; matrix products, arithmetic and copies ran while one was open for 0% of the time, Pallas kernels for 20%

profile of v3, /device:TPU:4, one launch (start us, length us, event | category | flops | bytes accessed | tf_op | source)
XLA Modules:
  0.0 87.7 jit_solution(2521321415794925748)
XLA Ops:
  0.6 0.0 copy-start.3
  0.6 0.0 copy-start.5
  0.7 0.0 copy-start.4
  0.7 3.6 %collective-permute-start = (f32[2,128]{1,0:T(2,128)}, f32[2,128]{1,0:T(2,128)S(1)}, u32[]{:S(2)}, u32[]{:S(2)}) collective-permute-start(f32[2,128]{1,0:T(2,128)} %tau_hbm.5), channel_id=1, source_target_pairs={{0,1},{1,2},{2,3},{3,4},{4,5},{5,6},{6,7},{7,8},{8,9},{9,10},{10,1... | collective-permute-start | bytes 3080 | tf_op jit(solution)/shard_map/ppermute | solution.py:497
  4.3 3.1 %collective-permute-done.side_ref = f32[2,128]{1,0:T(2,128)S(1)} collective-permute-done((f32[2,128]{1,0:T(2,128)}, f32[2,128]{1,0:T(2,128)S(1)}, u32[]{:S(2)}, u32[]{:S(2)}) %collective-permute-start) | collective-permute-done | bytes 1056 | tf_op jit(solution)/shard_map/ppermute | solution.py:497
  7.4 0.0 collective-permute-start.1
  7.4 0.0 copy-start.1
  7.4 0.7 copy-done.1
  8.1 0.0 copy-start.6
  8.1 0.0 copy-start.2
  8.1 4.9 %shard_map.80 = (f32[1736,128]{1,0:T(8,128)S(1)}, f32[760,128]{1,0:T(8,128)S(1)}, f32[976,128]{1,0:T(8,128)S(1)}, s32[128,128]{1,0:T(8,128)S(1)}, s32[48,128]{1,0:T(8,128)S(1)}) custom-call(f32[6912,128]{1,0:T(8,128)} %bitcast.9, s32[27,128]{1,0:T(8,128)S(1)} %bitcast.6), custom_call_target="tpu_custom_call" | custom-call | flops 1048576 | bytes 8388608 | tf_op jit(solution)/shard_map/pallas_call | solution.py:468
  13.0 2.6 %collective-permute-start.5 = (f32[1736,128]{1,0:T(8,128)S(1)}, f32[1736,128]{1,0:T(8,128)}, u32[]{:S(2)}, u32[]{:S(2)}) collective-permute-start(f32[1736,128]{1,0:T(8,128)S(1)} %get-tuple-element.21), channel_id=1, source_target_pairs={{0,1},{1,2},{2,3},{3,4},{4,5},{5,6},{6,7},{7,8},{8,9},{9,10},{10,1... | collective-permute-start | bytes 2666504 | tf_op jit(solution)/shard_map/ppermute | solution.py:505
  15.6 0.0 collective-permute-done.1.other_ref
  15.6 0.0 copy-done.3
  15.6 0.0 copy-done.5
  15.6 0.0 copy-done.4
  15.7 0.0 copy-done.6
  15.7 3.9 %shard_map.77.mine_hbm = f32[24,128]{1,0:T(8,128)S(1)} custom-call(f32[6912,128]{1,0:T(8,128)} %bitcast.10, s32[27,128]{1,0:T(8,128)S(1)} %bitcast.7, f32[2,128]{1,0:T(2,128)S(1)} %copy-done.3, f32[2,128]{1,0:T(2,128)S(1)} %collective-permute-done.side_ref, f32[2,128]{1,0:T(2,128)S(1)} %collective-permute-done.1.other_ref, s32[2,128]{1,0:T(2,128)S(1)} %copy-done.4, ...), custom_call_target="tpu_custom_call" | custom-call | flops 1073741824 | bytes 8388608 | tf_op jit(solution)/shard_map/pallas_call | solution.py:468
  19.6 0.3 collective-permute-start.2
  19.9 1.0 %collective-permute-done.2.other_hbm = f32[24,128]{1,0:T(8,128)S(1)} collective-permute-done((f32[24,128]{1,0:T(8,128)S(1)}, f32[24,128]{1,0:T(8,128)S(1)}, u32[]{:S(2)}, u32[]{:S(2)}) %collective-permute-start.2) | collective-permute-done | bytes 12320 | tf_op jit(solution)/shard_map/ppermute | solution.py:515
  20.8 0.8 shard_map.78
  21.7 18.3 %all-to-all-start = ((f32[128,1,768]{2,1,0:T(1,128)}), f32[128,1,768]{2,1,0:T(1,128)S(1)}, u32[]{:S(2)}, u32[]{:S(2)}) async-start(f32[128,1,768]{2,1,0:T(1,128)} %bitcast.2), calls=%async_computation | async-start | bytes 786432 | tf_op jit(solution)/shard_map/all_to_all | solution.py:522
  39.9 3.4 %collective-permute-start.7 = (f32[976,128]{1,0:T(8,128)S(1)}, f32[976,128]{1,0:T(8,128)S(1)}, u32[]{:S(2)}, u32[]{:S(2)}) collective-permute-start(f32[976,128]{1,0:T(8,128)S(1)} %get-tuple-element.23), channel_id=1, source_target_pairs={{1,0},{2,1},{3,2},{4,3},{5,4},{6,5},{7,6},{8,7},{9,8},{10,9},{11,1... | collective-permute-start | bytes 1499144 | tf_op jit(solution)/shard_map/ppermute | solution.py:524
  43.3 2.5 %collective-permute-start.6 = (f32[760,128]{1,0:T(8,128)S(1)}, f32[760,128]{1,0:T(8,128)S(1)}, u32[]{:S(2)}, u32[]{:S(2)}) collective-permute-start(f32[760,128]{1,0:T(8,128)S(1)} %get-tuple-element.22), channel_id=1, source_target_pairs={{1,0},{2,1},{3,2},{4,3},{5,4},{6,5},{7,6},{8,7},{9,8},{10,9},{11,1... | collective-permute-start | bytes 1167368 | tf_op jit(solution)/shard_map/ppermute | solution.py:506
  45.8 1.5 %collective-permute-start.3 = (f32[16,128]{1,0:T(8,128)S(1)}, f32[16,128]{1,0:T(8,128)S(1)}, u32[]{:S(2)}, u32[]{:S(2)}) collective-permute-start(f32[16,128]{1,0:T(8,128)S(1)} %get-tuple-element.14.mine_hbm), channel_id=1, source_target_pairs={{0,1},{1,128},{2,3},{3,130},{4,5},{5,132},{6,7},{7,134},{8,9},{9,1... | collective-permute-start | bytes 24584 | tf_op jit(solution)/shard_map/ppermute | solution.py:523
  47.3 3.5 %collective-permute-done.3 = f32[16,128]{1,0:T(8,128)S(1)} collective-permute-done((f32[16,128]{1,0:T(8,128)S(1)}, f32[16,128]{1,0:T(8,128)S(1)}, u32[]{:S(2)}, u32[]{:S(2)}) %collective-permute-start.3) | collective-permute-done | bytes 8224 | tf_op jit(solution)/shard_map/ppermute | solution.py:523
  50.8 17.8 %collective-permute-start.4 = (f32[16,128]{1,0:T(8,128)S(1)}, f32[16,128]{1,0:T(8,128)S(1)}, u32[]{:S(2)}, u32[]{:S(2)}) collective-permute-start(f32[16,128]{1,0:T(8,128)S(1)} %collective-permute-done.3), channel_id=1, source_target_pairs={{0,1},{1,128},{2,3},{3,130},{4,5},{5,132},{6,7},{7,134},{8,9},{9,1... | collective-permute-start | bytes 24584 | tf_op jit(solution)/shard_map/ppermute | solution.py:523
  68.6 3.3 %collective-permute-done.4.other_hbm = f32[16,128]{1,0:T(8,128)S(1)} collective-permute-done((f32[16,128]{1,0:T(8,128)S(1)}, f32[16,128]{1,0:T(8,128)S(1)}, u32[]{:S(2)}, u32[]{:S(2)}) %collective-permute-start.4) | collective-permute-done | bytes 8224 | tf_op jit(solution)/shard_map/ppermute | solution.py:523
  71.9 0.0 copy-done.2
  71.9 8.3 %shard_map.79 = (f32[6912,128]{1,0:T(8,128)}, f32[3456,128]{1,0:T(8,128)S(1)}, f32[128,128]{1,0:T(8,128)S(1)}) custom-call(f32[6912,128]{1,0:T(8,128)} %bitcast.11, s32[27,128]{1,0:T(8,128)S(1)} %bitcast.8, f32[16,128]{1,0:T(8,128)S(1)} %get-tuple-element.14.mine_hbm, f32[16,128]{1,0:T(8,128)S(1)} %collective-permute-done.4.other_hbm, ...), custom_call_target="tpu_custom_call" | custom-call | flops 1073741824 | bytes 8388608 | tf_op jit(solution)/shard_map/pallas_call | solution.py:468
  80.2 0.0 copy-start
  80.2 1.3 %copy-done = f32[3456,128]{1,0:T(8,128)} copy-done((f32[3456,128]{1,0:T(8,128)}, f32[3456,128]{1,0:T(8,128)S(1)}, u32[]{:S(2)}) %copy-start) | copy-done | bytes 1769496
  81.4 0.0 collective-permute-done.6.early_hbm
  81.5 0.0 collective-permute-done.7.late_hbm
  81.5 0.0 all-to-all-done
  81.5 0.0 collective-permute-done.5.up_hbm
  81.5 6.3 %shard_map.81 = (f32[6912,128]{1,0:T(8,128)}, f32[2,128]{1,0:T(2,128)}) custom-call(f32[6912,128]{1,0:T(8,128)} %get-tuple-element.15.pre_hbm, f32[3456,128]{1,0:T(8,128)} %copy-done, f32[128,128]{1,0:T(8,128)S(1)} %get-tuple-element.17.shape_hbm, s32[128,128]{1,0:T(8,128)S(1)} %get-tuple-element.18.dest_hbm, s32[48,128]{1,0:T(8,128)S(1)} %get-tuple-element.19.table_hbm, ...), custom_call_target="tpu_custom_call" | custom-call | flops 16777216 | bytes 8388608 | tf_op jit(solution)/shard_map/pallas_call | solution.py:468
Async XLA Ops:
  0.6 15.0 %copy-start.3 = (f32[2,128]{1,0:T(2,128)S(1)}, f32[2,128]{1,0:T(2,128)}, u32[]{:S(2)}) copy-start(f32[2,128]{1,0:T(2,128)} %tau_hbm.5) | copy-start | bytes 3076
  0.6 15.0 %copy-start.5 = (f32[2,128]{1,0:T(2,128)S(1)}, f32[2,128]{1,0:T(2,128)}, u32[]{:S(2)}) copy-start(f32[2,128]{1,0:T(2,128)} %heat_hbm.3) | copy-start | bytes 3076
  0.7 15.0 %copy-start.4 = (s32[2,128]{1,0:T(2,128)S(1)}, s32[2,128]{1,0:T(2,128)}, u32[]{:S(2)}) copy-start(s32[2,128]{1,0:T(2,128)} %wall_hbm.3) | copy-start | bytes 3076
  0.7 6.7 %collective-permute-start = (f32[2,128]{1,0:T(2,128)}, f32[2,128]{1,0:T(2,128)S(1)}, u32[]{:S(2)}, u32[]{:S(2)}) collective-permute-start(f32[2,128]{1,0:T(2,128)} %tau_hbm.5), channel_id=1, source_target_pairs={{0,1},{1,2},{2,3},{3,4},{4,5},{5,6},{6,7},{7,8},{8,9},{9,10},{10,1... | collective-permute-start | bytes 3080 | tf_op jit(solution)/shard_map/ppermute | solution.py:497
  7.4 8.2 %collective-permute-start.1 = (f32[2,128]{1,0:T(2,128)S(1)}, f32[2,128]{1,0:T(2,128)S(1)}, u32[]{:S(2)}, u32[]{:S(2)}) collective-permute-start(f32[2,128]{1,0:T(2,128)S(1)} %collective-permute-done.side_ref), channel_id=1, source_target_pairs={{0,64},{64,0},{1,65},{65,1},{2,66},{66,2},{3,67},{67,3},{4,68},{68... | collective-permute-start | bytes 3080 | tf_op jit(solution)/shard_map/ppermute | solution.py:507
  7.4 0.7 copy-start.1
  8.1 7.6 %copy-start.6 = (f32[8,24]{1,0:T(8,128)S(1)}, f32[8,24]{1,0:T(8,128)}, u32[]{:S(2)}) copy-start(f32[8,24]{1,0:T(8,128)} %constant.2.clone.c_hbm) | copy-start | bytes 2308
  8.1 63.8 %copy-start.2 = (s32[3456]{0:T(1024)S(1)}, s32[3456]{0:T(1024)}, u32[]{:S(2)}) copy-start(s32[3456]{0:T(1024)} %param.7) | copy-start | bytes 41476
  13.0 68.4 %collective-permute-start.5 = (f32[1736,128]{1,0:T(8,128)S(1)}, f32[1736,128]{1,0:T(8,128)}, u32[]{:S(2)}, u32[]{:S(2)}) collective-permute-start(f32[1736,128]{1,0:T(8,128)S(1)} %get-tuple-element.21), channel_id=1, source_target_pairs={{0,1},{1,2},{2,3},{3,4},{4,5},{5,6},{6,7},{7,8},{8,9},{9,10},{10,1... | collective-permute-start | bytes 2666504 | tf_op jit(solution)/shard_map/ppermute | solution.py:505
  19.6 1.3 %collective-permute-start.2 = (f32[24,128]{1,0:T(8,128)S(1)}, f32[24,128]{1,0:T(8,128)S(1)}, u32[]{:S(2)}, u32[]{:S(2)}) collective-permute-start(f32[24,128]{1,0:T(8,128)S(1)} %shard_map.77.mine_hbm), channel_id=1, source_target_pairs={{0,64},{64,0},{1,65},{65,1},{2,66},{66,2},{3,67},{67,3},{4,68},{68... | collective-permute-start | bytes 36872 | tf_op jit(solution)/shard_map/ppermute | solution.py:515
  21.7 59.8 %all-to-all-start = ((f32[128,1,768]{2,1,0:T(1,128)}), f32[128,1,768]{2,1,0:T(1,128)S(1)}, u32[]{:S(2)}, u32[]{:S(2)}) async-start(f32[128,1,768]{2,1,0:T(1,128)} %bitcast.2), calls=%async_computation | async-start | bytes 786432 | tf_op jit(solution)/shard_map/all_to_all | solution.py:522
  39.9 41.5 %collective-permute-start.7 = (f32[976,128]{1,0:T(8,128)S(1)}, f32[976,128]{1,0:T(8,128)S(1)}, u32[]{:S(2)}, u32[]{:S(2)}) collective-permute-start(f32[976,128]{1,0:T(8,128)S(1)} %get-tuple-element.23), channel_id=1, source_target_pairs={{1,0},{2,1},{3,2},{4,3},{5,4},{6,5},{7,6},{8,7},{9,8},{10,9},{11,1... | collective-permute-start | bytes 1499144 | tf_op jit(solution)/shard_map/ppermute | solution.py:524
  43.3 38.1 %collective-permute-start.6 = (f32[760,128]{1,0:T(8,128)S(1)}, f32[760,128]{1,0:T(8,128)S(1)}, u32[]{:S(2)}, u32[]{:S(2)}) collective-permute-start(f32[760,128]{1,0:T(8,128)S(1)} %get-tuple-element.22), channel_id=1, source_target_pairs={{1,0},{2,1},{3,2},{4,3},{5,4},{6,5},{7,6},{8,7},{9,8},{10,9},{11,1... | collective-permute-start | bytes 1167368 | tf_op jit(solution)/shard_map/ppermute | solution.py:506
  45.8 5.0 %collective-permute-start.3 = (f32[16,128]{1,0:T(8,128)S(1)}, f32[16,128]{1,0:T(8,128)S(1)}, u32[]{:S(2)}, u32[]{:S(2)}) collective-permute-start(f32[16,128]{1,0:T(8,128)S(1)} %get-tuple-element.14.mine_hbm), channel_id=1, source_target_pairs={{0,1},{1,128},{2,3},{3,130},{4,5},{5,132},{6,7},{7,134},{8,9},{9,1... | collective-permute-start | bytes 24584 | tf_op jit(solution)/shard_map/ppermute | solution.py:523
  50.8 21.1 %collective-permute-start.4 = (f32[16,128]{1,0:T(8,128)S(1)}, f32[16,128]{1,0:T(8,128)S(1)}, u32[]{:S(2)}, u32[]{:S(2)}) collective-permute-start(f32[16,128]{1,0:T(8,128)S(1)} %collective-permute-done.3), channel_id=1, source_target_pairs={{0,1},{1,128},{2,3},{3,130},{4,5},{5,132},{6,7},{7,134},{8,9},{9,1... | collective-permute-start | bytes 24584 | tf_op jit(solution)/shard_map/ppermute | solution.py:523
  80.2 1.3 %copy-start = (f32[3456,128]{1,0:T(8,128)}, f32[3456,128]{1,0:T(8,128)S(1)}, u32[]{:S(2)}) copy-start(f32[3456,128]{1,0:T(8,128)S(1)} %get-tuple-element.16.along_hbm) | copy-start | bytes 5308420
